TPU v7x, 128 devices: a whole 4x4x4 slice. The times are simulated.
128 devices in a mesh: seq: 8 (over z, core), tp: 16 (over x, y).
Axes of the slice: x: 4, y: 4, z: 4, core: 2. Of those that a mesh axis runs over, the one named last changes fastest.
Arguments:
- patches: bfloat16 [32768, 1280], P(('seq', 'tp')), may hold values from -6 to 6
- image_table: int32 [256, 3], replicated, may hold values from 0 to 4095, as said below
- ln_gain: float32 [1280], replicated, may hold values from 0.25 to 1.75
- ln_bias: float32 [1280], replicated, may hold values from -3 to 3
- merge_up: bfloat16 [5120, 5120], P(None, 'tp'), may hold values from -0.078125 to 0.078125
- merge_up_bias: float32 [5120], P('tp'), may hold values from -3 to 3
- merge_down: bfloat16 [5120, 3584], P('tp'), may hold values from -0.15625 to 0.15625
- merge_down_bias: float32 [3584], replicated, may hold values from -3 to 3
- text_embeds: bfloat16 [4096, 3584], P('seq', 'tp'), may hold values from -6 to 6
- attn_gain: float32 [3584], replicated, may hold values from 0.25 to 1.75
- q_weight: bfloat16 [3584, 2048], P(None, 'tp'), may hold values from -2 to 2
- q_bias: float32 [2048], P('tp'), may hold values from -3 to 3
- key_value_weight: bfloat16 [3584, 1024], replicated, may hold values from -2 to 2
- key_value_bias: float32 [1024], replicated, may hold values from -3 to 3
- o_weight: bfloat16 [2048, 3584], P('tp'), may hold values from -0.1875 to 0.1875
Outputs:
- block_out: bfloat16 [4096, 3584], P('seq', 'tp')
Inputs may be any that keep to these rules, and one draw needn't show every extreme that they name: `image_table`: grid entries are even. Table rows 2d and 2d + 1 are the two images of device d = seq index * 16 + tp index; the second starts right after the first, so the device's tokens fill consecutive positions inside block [s * 512, (s + 1) * 512) of its seq index s. Images never intersect. The two images of a device hold at most 64 merged tokens, and in every seq group one device holds exactly 64. A sequence block holds at most 424 image tokens, and some block holds exactly that many.
All inputs are finite; a program needn't handle non-finite values.
Results may differ from a plain program's by a relative error of at most 0.012.
Values may be sent and summed in bfloat16 or wider, within the bound.
A program may use at most 128 MiB of HBM per device.

v0:
```python
import jax
import jax.numpy as jnp
from jax import lax
from jax.sharding import PartitionSpec as P

HEAD_DIMENSION = 128
KEY_VALUE_HEADS = 4
LOCAL_QUERY_HEAD = 16
CAP = 64
TOK_SEQ = 512
MW = 5120


EPS = 1e-06
THETA = 1000000.0


def sent_together(arrays, axis, dim, along):
    both = jnp.concatenate(arrays, axis=along)
    out, at, done = (lax.all_gather(both, axis, axis=dim, tiled=True), 0, [])
    for a in arrays:
        done.append(lax.slice_in_dim(out, at, at + a.shape[along], axis=along))
        at += a.shape[along]
    return tuple(done)


def copy_for_each(shard, axis):
    peers = lax.axis_size(axis)
    return lax.all_to_all(
        jnp.broadcast_to(shard[None], (peers, *shard.shape)), axis, 0, 0, tiled=True
    )


def laid_out(pieces, dim):
    lengths = list(pieces.shape[1:])
    lengths[dim] *= pieces.shape[0]
    return jnp.moveaxis(pieces, 0, dim).reshape(lengths)


def gathered_copies(shard, axis, dim):
    pieces = copy_for_each(shard, axis)
    return laid_out(pieces, dim)


def layer_norm(row_data, scale_row, offset_row):
    centre = jnp.mean(row_data, axis=-1, keepdims=True)
    centred = row_data - centre
    spread = jnp.mean(centred * centred, axis=-1, keepdims=True)
    return centred * lax.rsqrt(spread + EPS) * scale_row + offset_row


def image_fields(image_table):
    grid_h = image_table[:, 0]
    grid_w = image_table[:, 1]
    across = grid_w // 2
    return (across, grid_h // 2 * across, image_table[:, 2])


def rope_tables(positions, image_table, head_size):
    across, counts, offsets = image_fields(image_table)
    inside = (
        (positions[:, None] >= offsets[None, :])
        & (positions[:, None] < (offsets + counts)[None, :])
    ).astype(jnp.int32)
    is_image = jnp.sum(inside, axis=1)
    run_start = jnp.sum(inside * offsets[None, :], axis=1)
    row_width = jnp.sum(inside * across[None, :], axis=1) + (1 - is_image)
    inner_index = positions - run_start
    pos_t = jnp.where(is_image > 0, run_start, positions)
    pos_h = jnp.where(is_image > 0, run_start + inner_index // row_width, positions)
    pos_w = jnp.where(is_image > 0, run_start + inner_index % row_width, positions)
    half_size = head_size // 2
    frequency = jnp.arange(half_size, dtype=jnp.int32)
    inverse = THETA ** (-2.0 * frequency.astype(jnp.float32) / head_size)
    first_cut = head_size // 8
    second_cut = first_cut + 3 * head_size // 16
    chosen = jnp.where(
        frequency[None, :] < first_cut,
        pos_t[:, None],
        jnp.where(frequency[None, :] < second_cut, pos_h[:, None], pos_w[:, None]),
    )
    angles = chosen.astype(jnp.float32) * inverse[None, :]
    angles = jnp.concatenate([angles, angles], axis=1)
    return (jnp.cos(angles), jnp.sin(angles), is_image)


def apply_rotation(value_tensor, cosine_values, sine_lookup):
    half_size = value_tensor.shape[-1] // 2
    turned = jnp.concatenate(
        [-value_tensor[..., half_size:], value_tensor[..., :half_size]], axis=-1
    )
    return value_tensor * cosine_values[:, None, :] + turned * sine_lookup[:, None, :]


def merger_hidden(vision, merge_up, merge_up_bias, image_weight):
    lifted = jnp.dot(vision, merge_up, preferred_element_type=jnp.float32) + merge_up_bias
    return (jax.nn.gelu(lifted, approximate=False) * image_weight[:, None]).astype(jnp.bfloat16)


def per_device(
    patches,
    image_table,
    ln_gain,
    ln_bias,
    merge_up,
    merge_up_bias,
    merge_down,
    merge_down_bias,
    text_embeds,
    attn_gain,
    q_weight,
    q_bias,
    key_value_weight,
    key_value_bias,
    o_weight,
):
    tp_count = lax.axis_size("tp")
    seq_index = lax.axis_index("seq")
    tensor_parallel_index = lax.axis_index("tp")
    row_share = TOK_SEQ // tp_count
    column_count = text_embeds.shape[1]
    local_heads = q_weight.shape[1] // HEAD_DIMENSION
    normed = layer_norm(patches.astype(jnp.float32), ln_gain, ln_bias).astype(jnp.bfloat16)
    merged = normed.reshape(CAP, MW)
    block_index = jnp.arange(TOK_SEQ, dtype=jnp.int32)
    positions = seq_index * TOK_SEQ + block_index % row_share * tp_count + block_index // row_share
    cosine_values, sine_lookup, is_image = rope_tables(positions, image_table, HEAD_DIMENSION)
    image_weight = is_image.astype(jnp.float32)
    across, counts, offsets = image_fields(image_table)
    group_begin = 2 * seq_index * tp_count
    group_first = lax.dynamic_slice_in_dim(offsets, group_begin, 2 * tp_count).reshape(tp_count, 2)[
        :, 0
    ]
    group_length = jnp.sum(
        lax.dynamic_slice_in_dim(counts, group_begin, 2 * tp_count).reshape(tp_count, 2), axis=1
    )
    run_start = group_first[tensor_parallel_index]
    run_length = group_length[tensor_parallel_index]
    per_peer = CAP // tp_count + 1
    residue = run_start % tp_count
    slot_index = (
        jnp.arange(tp_count, dtype=jnp.int32)[:, None]
        + jnp.arange(per_peer, dtype=jnp.int32)[None, :] * tp_count
        - residue
    ).reshape(-1)
    live_slot = (slot_index >= 0) & (slot_index < run_length)
    picker = (
        (slot_index[:, None] == jnp.arange(CAP, dtype=jnp.int32)[None, :]) & live_slot[:, None]
    ).astype(jnp.bfloat16)
    outgoing = (
        jnp.dot(picker, merged, preferred_element_type=jnp.float32)
        .astype(jnp.bfloat16)
        .reshape(tp_count, per_peer, MW)
    )
    incoming = lax.all_to_all(outgoing, "tp", split_axis=0, concat_axis=0, tiled=True)
    target = (
        group_first[:, None] // tp_count
        - seq_index * row_share
        + jnp.arange(per_peer, dtype=jnp.int32)[None, :]
    ).reshape(-1)
    placer = (target[None, :] == jnp.arange(row_share, dtype=jnp.int32)[:, None]).astype(
        jnp.bfloat16
    )
    own_rows = jnp.dot(
        placer, incoming.reshape(tp_count * per_peer, MW), preferred_element_type=jnp.float32
    ).astype(jnp.bfloat16)
    weight_rows = image_weight
    hidden = merger_hidden(
        lax.all_gather(own_rows, "tp", axis=0, tiled=True), merge_up, merge_up_bias, weight_rows
    )
    partial_sum = jnp.dot(hidden, merge_down, preferred_element_type=jnp.float32)
    text_rows = (
        text_embeds.reshape(row_share, tp_count, column_count)
        .transpose(1, 0, 2)
        .reshape(TOK_SEQ, column_count)
        .astype(jnp.float32)
    )
    text_rows = text_rows * (1.0 - image_weight)[:, None]
    column_start = tensor_parallel_index * column_count
    single_key_head = tensor_parallel_index * local_heads // (LOCAL_QUERY_HEAD // KEY_VALUE_HEADS)
    key_weight = lax.dynamic_slice_in_dim(
        key_value_weight, single_key_head * HEAD_DIMENSION, HEAD_DIMENSION, 1
    )
    value_matrix = lax.dynamic_slice_in_dim(
        key_value_weight,
        KEY_VALUE_HEADS * HEAD_DIMENSION + single_key_head * HEAD_DIMENSION,
        HEAD_DIMENSION,
        1,
    )
    key_bias = lax.dynamic_slice_in_dim(
        key_value_bias, single_key_head * HEAD_DIMENSION, HEAD_DIMENSION
    )
    bias_of_value = lax.dynamic_slice_in_dim(
        key_value_bias,
        KEY_VALUE_HEADS * HEAD_DIMENSION + single_key_head * HEAD_DIMENSION,
        HEAD_DIMENSION,
    )
    current = lax.dynamic_slice_in_dim(partial_sum, column_start, column_count, 1)
    term = lax.dynamic_update_slice_in_dim(partial_sum, current + text_rows, column_start, 1)
    summed = lax.psum(term, "tp")
    residual = summed + image_weight[:, None] * merge_down_bias[None, :]
    scale_rows = lax.rsqrt(jnp.mean(residual * residual, axis=1) + EPS)
    normed_rows = (residual * scale_rows[:, None] * attn_gain[None, :]).astype(jnp.bfloat16)
    query = jnp.dot(normed_rows, q_weight, preferred_element_type=jnp.float32)
    key_tensor = jnp.dot(normed_rows, key_weight, preferred_element_type=jnp.float32)
    value_tensor = jnp.dot(normed_rows, value_matrix, preferred_element_type=jnp.float32)
    residual_columns = lax.dynamic_slice_in_dim(residual, column_start, column_count, 1)
    query = apply_rotation(
        (query + q_bias).reshape(TOK_SEQ, local_heads, HEAD_DIMENSION), cosine_values, sine_lookup
    ).astype(jnp.bfloat16)
    key_tensor = (
        apply_rotation(
            (key_tensor + key_bias).reshape(TOK_SEQ, 1, HEAD_DIMENSION), cosine_values, sine_lookup
        )
        .reshape(TOK_SEQ, HEAD_DIMENSION)
        .astype(jnp.bfloat16)
    )
    value_tensor = (value_tensor + bias_of_value).astype(jnp.bfloat16)
    score_scale = HEAD_DIMENSION ** (-0.5)
    best_score = jnp.full((local_heads, TOK_SEQ), -1e30, jnp.float32)
    key_piece, value_piece = sent_together((key_tensor, value_tensor), "seq", 0, 1)
    global_row = jnp.arange(key_piece.shape[0], dtype=jnp.int32)
    inner_row = global_row % TOK_SEQ
    key_position = (
        global_row // TOK_SEQ * TOK_SEQ + inner_row % row_share * tp_count + inner_row // row_share
    )
    scores = (
        jnp.einsum("qhd,kd->hqk", query, key_piece, preferred_element_type=jnp.float32)
        * score_scale
    )
    allowed = key_position[None, None, :] <= positions[None, :, None]
    scores = jnp.where(allowed, scores, -1e30)
    fresh_best = jnp.maximum(best_score, jnp.max(scores, axis=2))
    weights = jnp.where(allowed, jnp.exp(scores - fresh_best[:, :, None]), 0.0)
    total_weight = jnp.sum(weights, axis=2)
    accumulated = jnp.einsum(
        "hqk,kd->hqd", weights.astype(jnp.bfloat16), value_piece, preferred_element_type=jnp.float32
    )
    best_score, total_weight, accumulated = (fresh_best, total_weight, accumulated)
    attention = (
        (accumulated / total_weight[:, :, None])
        .astype(jnp.bfloat16)
        .transpose(1, 0, 2)
        .reshape(TOK_SEQ, local_heads * HEAD_DIMENSION)
    )
    weight_cols = lax.all_to_all(o_weight, "tp", split_axis=1, concat_axis=0, tiled=True)
    weight_rows = weight_cols
    mixed = jnp.dot(
        gathered_copies(attention, "tp", 1), weight_rows, preferred_element_type=jnp.float32
    )
    output_rows = residual_columns + mixed
    return (
        output_rows.reshape(tp_count, row_share, column_count)
        .transpose(1, 0, 2)
        .reshape(TOK_SEQ, column_count)
        .astype(jnp.bfloat16)
    )


def solution(mesh):
    return jax.shard_map(
        per_device,
        mesh=mesh,
        in_specs=(
            P(("seq", "tp"), None),
            P(),
            P(),
            P(),
            P(None, "tp"),
            P("tp"),
            P("tp", None),
            P(),
            P("seq", "tp"),
            P(),
            P(None, "tp"),
            P("tp"),
            P(),
            P(),
            P("tp", None),
        ),
        out_specs=P("seq", "tp"),
        check_vma=False,
    )
```

profile of v0, /device:TPU:96, one launch (start us, length us, event | category | flops | bytes accessed | tf_op | source)
XLA Modules:
  0.0 351.9 jit_solution(4391008567551796274)
XLA Ops:
  6.5 0.9 fusion.178
  7.4 0.1 fusion.140
  7.5 0.1 reshape.439
  7.6 0.1 fusion.118
  7.7 0.5 constant_dynamic-slice_fusion
  10.2 0.1 sub.119
  10.3 0.1 dynamic_slice.32
  10.4 0.1 reshape.440
  10.5 0.1 reduce_sum.72
  10.6 0.6 dynamic_slice.33
  11.2 1.3 convert_reduce_fusion
  12.5 1.4 fusion.10
  13.9 2.3 fusion.13
  16.2 2.3 reshape.441
  18.4 0.6 compare_and_fusion.1
  19.1 2.4 convolution_convert_fusion
  21.5 2.3 reshape.442
  23.8 7.1 %all-to-all-start = ((bf16[16,5,5120]{2,1,0:T(8,128)(2,1)}), bf16[16,5,5120]{2,1,0:T(8,128)(2,1)}, u32[]{:S(2)}, u32[]{:S(2)}) async-start(bf16[16,5,5120]{2,1,0:T(8,128)(2,1)} %reshape.442), calls=%async_computation | async-start | bytes 2621440 | tf_op jit(solution)/shard_map/all_to_all | solution.py:155
  30.9 0.0 all-gather.3.cloned.1.call-start
  30.9 0.1 iota_add_fusion
  31.0 0.1 add.345
  31.1 20.6 %all-to-all-done = bf16[16,5,5120]{2,1,0:T(8,128)(2,1)} async-done(((bf16[16,5,5120]{2,1,0:T(8,128)(2,1)}), bf16[16,5,5120]{2,1,0:T(8,128)(2,1)}, u32[]{:S(2)}, u32[]{:S(2)}) %all-to-all-start) | async-done | bytes 819232 | tf_op jit(solution)/shard_map/all_to_all | solution.py:155
  51.7 2.2 reshape.443
  54.0 2.1 convolution_convert_fusion.1
  56.1 0.0 all-gather.3.cloned.1.call-update
  56.1 0.0 all-reduce.2.cloned.1.call-start
  56.1 1.1 copy.26
  57.3 1.1 copy.27
  58.4 0.4 select_reduce_fusion
  58.8 0.1 fusion.126
  59.0 51.1 %all-gather.3.cloned.1.call-done = bf16[512,5120]{1,0:T(8,128)(2,1)} async-done(((bf16[32,5120]{1,0:T(8,128)(2,1)}), bf16[512,5120]{1,0:T(8,128)(2,1)}) %all-gather.3.cloned.1.call-update) | async-done | bytes 5242896 | tf_op jit(solution)/shard_map/all_gather | solution.py:169
  110.1 11.4 %fusion.47 = f32[512,3584]{1,0:T(8,128)} fusion(bf16[320,3584]{1,0:T(8,128)(2,1)} %param.21, bf16[512,5120]{1,0:T(8,128)(2,1)} %all-gather.3.cloned.1.call-done, bf16[5120,320]{0,1:T(8,128)(2,1)S(1)} %copy-done, f32[512]{0:T(512)S(1)} %get-tuple-element.28, f32[320]{0:T(512)S(1)} %copy-done.10), kind=kOutput, calls=%fused_computation.58 | convolution fusion | flops 2863104000 | bytes 18156800 | tf_op jit(solution)/shard_map/dot_general | solution.py:171
  121.5 1.6 fusion.48
  123.1 3.5 %dynamic_update_slice.3 = f32[512,3584]{1,0:T(8,128)} dynamic-update-slice(f32[512,3584]{1,0:T(8,128)} %fusion.47, f32[512,224]{1,0:T(8,128)S(1)} %fusion.48, s32[]{:T(128)} %constant.213.clone.1, s32[]{:T(128)S(6)} %select_n.205) | dynamic-update-slice | bytes 917508 | tf_op jit(solution)/shard_map/dynamic_update_slice | solution.py:199
  126.6 0.0 all-reduce.2.cloned.1.call-update
  126.6 0.2 all-gather.5.cloned.1.call-start
  126.9 0.8 fusion.177
  127.7 0.1 convert_multiply_fusion
  127.8 0.0 copy-start.7
  127.9 130.4 %all-reduce.2.cloned.1.call-done = f32[512,3584]{1,0:T(8,128)} async-done(((f32[512,3584]{1,0:T(8,128)}), f32[512,3584]{1,0:T(8,128)}) %all-reduce.2.cloned.1.call-update) | async-done | bytes 7340048 | tf_op jit(solution)/shard_map/psum | solution.py:200
  258.3 4.2 %multiply_reduce_fusion = (f32[512]{0:T(512)S(1)}, f32[512,3584]{1,0:T(8,128)S(1)}) fusion(f32[512,3584]{1,0:T(8,128)} %all-reduce.2.cloned.1.call-done, f32[3584]{0:T(1024)S(1)} %copy-done.6, f32[512]{0:T(512)S(1)} %get-tuple-element.28), kind=kLoop, calls=%fused_computation.3 | loop fusion | flops 7339520 | bytes 14698496 | tf_op jit(solution)/shard_map/reduce_sum | solution.py:202
  262.5 1.1 multiply_convert_fusion
  263.6 1.8 copy-done.3
  265.5 3.2 convolution_add_fusion.3
  268.7 0.0 copy-start.4
  268.7 0.0 copy-start.5
  268.8 0.0 copy-start.8
  268.8 2.6 fusion.23
  271.4 1.0 fusion.88
  272.4 0.7 pad_maximum_fusion.1
  273.2 0.0 all-gather.5.cloned.1.call-update
  273.2 1.3 copy.28
  274.5 5.4 %all-to-all-start.2 = ((bf16[128,16,224]{0,2,1:T(8,128)(2,1)}), bf16[128,16,224]{0,2,1:T(8,128)(2,1)}, u32[]{:S(2)}, u32[]{:S(2)}) async-start(bf16[128,16,224]{0,2,1:T(8,128)(2,1)} %bitcast.18), calls=%async_computation.2 | async-start | bytes 1835008 | tf_op jit(solution)/shard_map/all_to_all | solution.py:246
  280.0 3.4 convolution_add_fusion.1
  283.4 13.4 %all-gather.5.cloned.1.call-done = bf16[4096,256]{0,1:T(8,128)(2,1)} async-done(((bf16[512,256]{0,1:T(8,128)(2,1)}), bf16[4096,256]{0,1:T(8,128)(2,1)}) %all-gather.5.cloned.1.call-update) | async-done | bytes 2097168 | tf_op jit(solution)/shard_map/all_gather | solution.py:20
  296.8 3.8 %fusion = (f32[512]{0:T(512)S(1)}, f32[4096,512]{1,0:T(8,128)S(1)}) fusion(s32[512]{0:T(512)S(1)} %fusion.123, s32[4096]{0:T(1024)S(1)} %fusion.106, f32[512,64]{0,1:T(8,128)S(1)} %convert_multiply_fusion, f32[512,128]{0,1:T(8,128)S(1)} %convolution_add_fusion.1, f32[512,64]{0,1:T(8,128)S(1)} %get-tuple-element.16, f32[512,64]{0,1:T(8,128)S(1)} %get-tuple-element.15, ...), kind=kOutput, calls=%fused_computation.5 | convolution fusion | flops 545652224 | bytes 10113024 | tf_op jit(solution)/shard_map/qhd,kd->hqk/dot_general | solution.py:228
  300.6 2.9 fusion.1
  303.5 0.0 copy-start.1
  303.5 3.0 fusion.27
  306.5 0.4 broadcast_in_dim.60
  306.9 35.3 %all_to_all.26 = bf16[16,512,128]{2,1,0:T(8,128)(2,1)S(1)} all-to-all(bf16[16,512,128]{2,1,0:T(8,128)(2,1)S(1)} %broadcast_in_dim.60), channel_id=1, replica_groups=mesh['seq'=8,'tp'=16] {'tp'}, dimensions={0} | all-to-all | bytes 4194304 | tf_op jit(solution)/shard_map/all_to_all | solution.py:29
  342.3 2.1 fusion.20
  344.4 0.2 copy.30
  344.6 0.8 copy.31
  (33 shorter events, 0.2 us)
Async XLA Ops:
  6.5 103.6 %copy-start = (bf16[5120,320]{0,1:T(8,128)(2,1)S(1)}, bf16[5120,320]{0,1:T(8,128)(2,1)}, u32[]{:S(2)}) copy-start(bf16[5120,320]{0,1:T(8,128)(2,1)} %param.19) | copy-start | bytes 9830404
  21.5 88.6 %copy-start.10 = (f32[320]{0:T(512)S(1)}, f32[320]{0:T(512)}, u32[]{:S(2)}) copy-start(f32[320]{0:T(512)} %param.20) | copy-start | bytes 3844
  23.8 27.9 %all-to-all-start = ((bf16[16,5,5120]{2,1,0:T(8,128)(2,1)}), bf16[16,5,5120]{2,1,0:T(8,128)(2,1)}, u32[]{:S(2)}, u32[]{:S(2)}) async-start(bf16[16,5,5120]{2,1,0:T(8,128)(2,1)} %reshape.442), calls=%async_computation | async-start | bytes 2621440 | tf_op jit(solution)/shard_map/all_to_all | solution.py:155
  30.9 79.2 %all-gather.3.cloned.1.call-start = ((), (), s32[]{:S(2)}) async-start(), calls=%async_computation.3 | async-start | bytes 5570560 | tf_op jit(solution)/shard_map/all_gather | solution.py:169
  56.1 202.2 %all-reduce.2.cloned.1.call-start = ((), (), s32[]{:S(2)}) async-start(), calls=%async_computation.4 | async-start | bytes 14680064 | tf_op jit(solution)/shard_map/psum | solution.py:200
  121.5 136.8 %copy-start.6 = (f32[3584]{0:T(1024)S(1)}, f32[3584]{0:T(1024)}, u32[]{:S(2)}) copy-start(f32[3584]{0:T(1024)} %param.22) | copy-start | bytes 43012
  126.6 170.2 %all-gather.5.cloned.1.call-start = ((), (), s32[]{:S(2)}) async-start(), calls=%async_computation.5 | async-start | bytes 2359296 | tf_op jit(solution)/shard_map/all_gather | solution.py:20
  127.8 134.7 %copy-start.7 = (f32[3584]{0:T(1024)S(1)}, f32[3584]{0:T(1024)}, u32[]{:S(2)}) copy-start(f32[3584]{0:T(1024)} %param.24) | copy-start | bytes 43012
  262.5 3.0 copy-start.3
  265.5 5.9 %copy-start.2 = (bf16[512,3584]{1,0:T(8,128)(2,1)}, bf16[512,3584]{1,0:T(8,128)(2,1)S(1)}, u32[]{:S(2)}) copy-start(bf16[512,3584]{1,0:T(8,128)(2,1)S(1)} %multiply_convert_fusion) | copy-start | bytes 11010052
  268.7 4.5 %copy-start.4 = (bf16[128,3584]{1,0:T(8,128)(2,1)S(1)}, bf16[128,3584]{1,0:T(8,128)(2,1)}, u32[]{:S(2)}) copy-start(bf16[128,3584]{1,0:T(8,128)(2,1)} %param.29) | copy-start | bytes 2752516
  268.7 11.2 %copy-start.5 = (bf16[3584,128]{1,0:T(8,128)(2,1)S(1)}, bf16[3584,128]{1,0:T(8,128)(2,1)}, u32[]{:S(2)}) copy-start(bf16[3584,128]{1,0:T(8,128)(2,1)} %param.25) | copy-start | bytes 2752516
  268.8 11.2 %copy-start.8 = (f32[128]{0:T(128)S(1)}, f32[128]{0:T(128)}, u32[]{:S(2)}) copy-start(f32[128]{0:T(128)} %param.26) | copy-start | bytes 1540
  274.5 32.0 %all-to-all-start.2 = ((bf16[128,16,224]{0,2,1:T(8,128)(2,1)}), bf16[128,16,224]{0,2,1:T(8,128)(2,1)}, u32[]{:S(2)}, u32[]{:S(2)}) async-start(bf16[128,16,224]{0,2,1:T(8,128)(2,1)} %bitcast.18), calls=%async_computation.2 | async-start | bytes 1835008 | tf_op jit(solution)/shard_map/all_to_all | solution.py:246
  300.6 2.9 copy-start.9
  303.5 41.9 %copy-start.1 = (bf16[5120,320]{0,1:T(8,128)(2,1)S(1)}, bf16[5120,320]{0,1:T(8,128)(2,1)}, u32[]{:S(2)}) copy-start(bf16[5120,320]{0,1:T(8,128)(2,1)} %param.19) | copy-start | bytes 9830404
Sparse Core Ops, SparseCore 0:
  56.2 53.8 all-gather.2
  126.7 131.4 all-reduce.1
  273.3 23.4 all-gather.4
where the time goes:
time: 356 us; the launch traced here: 352 us
  waiting for transfers between devices  216 us (61%)
  blocking collectives  35.3 us (10%)
  matrix products  34.1 us (10%)
  local copies, waits for them, and re-layouts  20.4 us (6%)
  other arithmetic  18.2 us (5%)
  between operations  15.5 us (4%)
  starting transfers between devices  12.8 us (4%)
    psum x1, waiting for transfers between devices, per_device(): summed = lax.psum(term, 'tp')  130 us
    all_gather x1, waiting for transfers between devices, per_device(): lax.all_gather(own_rows, 'tp', axis=0, tiled=True)  51.1 us
    all_to_all x1, blocking collectives, copy_for_each(): lax.all_to_all(jnp.broadcast_to(shard[None], (peers, *shard.shape)), axis...  35.3 us
    all_to_all x1, waiting for transfers between devices, per_device(): lax.all_to_all(outgoing, 'tp', split_axis=0, concat_axis=0, tiled=True)  20.6 us
    all_gather x1, waiting for transfers between devices, sent_together(): out, at, done = (lax.all_gather(both, axis, axis=dim, tiled=True), 0, [])  13.4 us
    dot_general x1, matrix products, per_device(): jnp.dot(hidden, merge_down, preferred_element_type=jnp.float32)  11.4 us
  transfers between devices with their start and end apart: 5, of which 4 were waited for; matrix products, arithmetic and copies ran while one was open for 5% of the time, Pallas kernels for 0%

commit v1 on v0

v1 whole, which is shorter than its diff:
```python
import functools

import jax
import jax.numpy as jnp
from jax import lax
from jax.experimental import pallas as pl
from jax.experimental.pallas import tpu as pltpu
from jax.sharding import PartitionSpec as P

MESH = pl.DeviceIdType.MESH
HEAD_DIMENSION = 128
KEY_VALUE_HEADS = 4
LOCAL_QUERY_HEAD = 16
CAP = 64
TOK_SEQ = 512
MW = 5120
VW = 1280
WIDTH = 3584
HID = 320
COLS = 224
N_TP = 16
N_SEQ = 8
SIDE = 4
ROWS = 448
HALF = 112
TCOL = 640
BLK = 896
RB = 128

EPS = 1e-06
THETA = 1000000.0
F32 = jnp.float32
BF16 = jnp.bfloat16


def al(value, multiple):
    return pl.multiple_of(value, multiple)


def place():
    t = lax.axis_index("tp")
    return t, t // SIDE, lax.rem(t, SIDE)


def wrap(value):
    return lax.rem(value + 2 * SIDE, SIDE)


def at_xy(x, y):
    return wrap(x) * SIDE + wrap(y)


def offset_xy(half, i, j):
    t, x, y = place()
    return (wrap(x + j), wrap(y + i)) if half == 0 else (wrap(x + i), wrap(y + j))


def peer(half, phase, sign):
    x, y = offset_xy(half, sign, 0) if phase == 1 else offset_xy(half, 0, sign)
    return x * SIDE + y


class Link:
    def __init__(self, send_sem, recv_sem, axis="tp"):
        self.send_sem, self.recv_sem, self.axis = send_sem, recv_sem, axis
        self.number, self.open = {}, []

    def _copy(self, key, src, dst, device):
        k = self.number.setdefault(key, len(self.number))
        return pltpu.make_async_remote_copy(
            src_ref=src,
            dst_ref=dst,
            send_sem=self.send_sem.at[k],
            recv_sem=self.recv_sem.at[k],
            device_id={self.axis: device},
            device_id_type=MESH,
        )

    def send(self, key, src, dst, device):
        copy = self._copy(key, src, dst, device)
        copy.start()
        self.open.append(copy)

    def arrived(self, key, dst, device):
        self._copy(key, dst, dst, device).wait_recv()

    def drain(self):
        assert len(self.number) <= self.send_sem.shape[0]
        for copy in self.open:
            copy.wait_send()
        self.open = []


def greet(devices, axis="tp"):
    barrier = pltpu.get_barrier_semaphore()
    for device in devices:
        pl.semaphore_signal(barrier, inc=1, device_id={axis: device}, device_id_type=MESH)
    pl.semaphore_wait(barrier, len(devices))


def ring_peers():
    return [peer(0, 1, 1), peer(0, 1, -1), peer(0, 2, 1), peer(0, 2, -1)]


def all_gather_2d(link, region):
    def reg(half, i, j, part):
        x, y = offset_xy(half, i, j)
        return region(half, x, y, part)

    def send(key, half, phase, sign, i, j, part):
        ref = reg(half, i, j, part)
        link.send((half, *key), ref, ref, peer(half, phase, sign))

    def got(key, half, phase, sign, i, j, part):
        link.arrived((half, *key), reg(half, i, j, part), peer(half, phase, -sign))

    both = ((1, 0), (-1, 1))
    halves = (0, 1)
    for h in halves:
        for s, _ in both:
            send(("p1", s), h, 1, s, 0, 0, None)
    for h in halves:
        for s, _ in both:
            send(("p2", s, 0), h, 2, s, 0, 0, None)
    for s, part in both:
        for h in halves:
            got(("p1", s), h, 1, s, -s, 0, None)
            send(("r1", s), h, 1, s, -s, 0, part)
            for s2, _ in both:
                send(("p2", s2, -s), h, 2, s2, -s, 0, None)
    for s, part in both:
        for h in halves:
            got(("p2", s, 0), h, 2, s, 0, -s, None)
            send(("r2", s, 0), h, 2, s, 0, -s, part)
    for s, part in both:
        for h in halves:
            got(("r1", s), h, 1, s, 2, 0, part)
            for s2, _ in both:
                send(("p2", s2, 2, part), h, 2, s2, 2, 0, part)
    for i in (-1, 1):
        for s, part in both:
            for h in halves:
                got(("p2", s, i), h, 2, s, i, -s, None)
                send(("r2", s, i), h, 2, s, i, -s, part)
    for s, part in both:
        for h in halves:
            got(("p2", s, 2, part), h, 2, s, 2, -s, part)
            send(("r2", s, 2), h, 2, s, 2, -s, part)
    for s, part in both:
        for h in halves:
            got(("p2", s, 2, 1 - part), h, 2, s, 2, -s, 1 - part)
    for i in (0, -1, 1, 2):
        for s, part in both:
            for h in halves:
                got(("r2", s, i), h, 2, s, i, 2, part)


AG_SEMS = 44


def tokens_kernel(patches, gain, bias, src_row, target, out, outgoing, incoming, send_sem, recv_sem):
    t, x, y = place()
    greet([lax.rem(t + o, N_TP) for o in range(1, N_TP)])
    link = Link(send_sem, recv_sem)
    rows = patches[...].astype(F32)
    centre = jnp.mean(rows, axis=-1, keepdims=True)
    centred = rows - centre
    spread = jnp.mean(centred * centred, axis=-1, keepdims=True)
    normed = (centred * lax.rsqrt(spread + EPS) * gain[...] + bias[...]).astype(BF16)
    lane = lax.broadcasted_iota(jnp.int32, (CAP, 4 * CAP), 1)
    for q in range(4):
        pick = (lane == src_row[...] + q).astype(BF16)
        part = jnp.dot(pick, normed, preferred_element_type=F32).astype(BF16)
        for u in range(2):
            for r in range(2):
                outgoing[2 * (2 * q + u) + r] = part[r * 32 : (r + 1) * 32, u * TCOL : (u + 1) * TCOL]
    for o in range(1, N_TP):
        to = lax.rem(t + o, N_TP)
        link.send(("a", o), outgoing.at[to], incoming.at[t], to)
    incoming[t] = outgoing[t]
    for o in range(1, N_TP):
        frm = lax.rem(t - o + N_TP, N_TP)
        link.arrived(("a", o), incoming.at[frm], frm)
    slots = incoming[...].reshape(N_TP * 32, TCOL)
    pick = (lax.broadcasted_iota(jnp.int32, (2 * HALF, N_TP * 32), 0) == target[...]).astype(BF16)
    mine = jnp.dot(pick, slots, preferred_element_type=F32).astype(BF16)
    out[pl.ds(al(lax.rem(t, 2) * 2 * HALF, 2 * HALF), 2 * HALF), pl.ds(al(t // 2 * TCOL, 128), TCOL)] = mine

    def region(half, x, y, part):
        d = x * SIDE + y
        first, width = ((0, TCOL), (0, 384), (384, 256))[0 if part is None else 1 + part]
        return out.at[
            pl.ds(al(lax.rem(d, 2) * 2 * HALF + half * HALF, 16), HALF),
            pl.ds(al(d // 2 * TCOL + first, 128), width),
        ]

    all_gather_2d(link, region)
    link.drain()


def gather_tokens(patches, gain, bias, src_row, target):
    vmem = pl.BlockSpec(memory_space=pltpu.VMEM)
    return pl.pallas_call(
        tokens_kernel,
        out_shape=jax.ShapeDtypeStruct((ROWS, MW), BF16),
        in_specs=[vmem] * 5,
        out_specs=vmem,
        scratch_shapes=[
            pltpu.VMEM((N_TP, 32, TCOL), BF16),
            pltpu.VMEM((N_TP, 32, TCOL), BF16),
            pltpu.SemaphoreType.DMA((AG_SEMS + N_TP,)),
            pltpu.SemaphoreType.DMA((AG_SEMS + N_TP,)),
        ],
        compiler_params=pltpu.CompilerParams(collective_id=0, has_side_effects=True),
        name="tokens",
    )(patches, gain, bias, src_row, target)


def merger_kernel(
    tokens, up, up_bias, src, down, text, out,
    lifted, hidden, part_ref,
    a_raw, a_mid, a_out, a_sum, b_raw, b_mid, b_out, b_sum,
    c_raw, c_mid, c_out, send_sem, recv_sem,
):
    t, x, y = place()
    greet(ring_peers())
    link = Link(send_sem, recv_sem)
    lifted[...] = jnp.zeros_like(lifted)

    def lift(k, carry):
        cols = pl.ds(al(k * TCOL, 128), TCOL)
        lifted[...] += jnp.dot(tokens[:, cols], up[cols, :], preferred_element_type=F32)
        return carry

    lax.fori_loop(0, MW // TCOL, lift, 0)
    raised = lifted[...] + up_bias[...]
    act = (0.5 * raised * (1.0 + lax.erf(raised * 0.5**0.5))).astype(BF16)
    pick = (lax.broadcasted_iota(jnp.int32, (TOK_SEQ, ROWS), 1) == src[...]).astype(BF16)
    hidden[...] = jnp.dot(pick, act, preferred_element_type=F32).astype(BF16)

    def lower(i, carry):
        for rb in range(SIDE):
            got = jnp.dot(hidden[rb * RB : (rb + 1) * RB, :], down[:, pl.ds(al(i * BLK, 128), BLK)], preferred_element_type=F32)
            part_ref[rb, :, pl.ds(al(i * BLK, 128), BLK)] = got.astype(BF16)
        return carry

    lax.fori_loop(0, SIDE, lower, 0)
    spot = (
        lax.broadcasted_iota(jnp.int32, (COLS, BLK), 0) + y * COLS == lax.broadcasted_iota(jnp.int32, (COLS, BLK), 1)
    ).astype(BF16)
    own = pl.ds(al(x * BLK, 128), BLK)
    for rb in range(SIDE):
        add = jnp.dot(text[rb * RB : (rb + 1) * RB, :], spot, preferred_element_type=F32)
        part_ref[rb, :, own] = (part_ref[rb, :, own].astype(F32) + add).astype(BF16)
    half_rows = RB // 2

    def a_piece(i, part):
        rows = (pl.ds(0, SIDE), pl.ds(0, 2), pl.ds(2, 2))[0 if part is None else 1 + part]
        return part_ref.at[rows, pl.ds(0, half_rows), pl.ds(al(wrap(x + i) * BLK, 128), BLK)]

    def b_piece(i, part):
        cols = (pl.ds(0, WIDTH), pl.ds(0, WIDTH // 2), pl.ds(WIDTH // 2, WIDTH // 2))[0 if part is None else 1 + part]
        return part_ref.at[wrap(y + i), pl.ds(half_rows, half_rows), cols]

    def to_x(s):
        return at_xy(x + s, y)

    def to_y(s):
        return at_xy(x, y + s)

    def mid_of(ref, name, part):
        if name == "a":
            return ref.at[pl.ds(2 * part, 2)]
        return ref.at[:, pl.ds(part * (WIDTH // 2), WIDTH // 2)]

    sides = (("a", a_piece, a_raw, a_mid, a_out, to_x), ("b", b_piece, b_raw, b_mid, b_out, to_y))
    signs = ((1, 0), (-1, 1))
    for n, piece, raw, mid, outb, to in sides:
        for s, part in signs:
            link.send((n, "raw", s), piece(2, part), raw.at[part], to(s))
    for n, piece, raw, mid, outb, to in sides:
        for s, part in signs:
            link.send((n, "own", s), piece(s, 1 - part), mid_of(mid.at[part], n, 1 - part), to(s))
    for n, piece, raw, mid, outb, to in sides:
        for s, part in signs:
            link.arrived((n, "raw", s), raw.at[part], to(-s))
            outb[part] = (raw[part].astype(F32) + piece(s, part)[...].astype(F32)).astype(BF16)
            link.send((n, "sum", s), outb.at[part], mid_of(mid.at[part], n, part), to(s))
    for n, piece, raw, mid, outb, to in sides:
        for s, part in signs:
            link.arrived((n, "own", s), mid_of(mid.at[part], n, 1 - part), to(-s))
            link.arrived((n, "sum", s), mid_of(mid.at[part], n, part), to(-s))
    a_sum[...] = (a_piece(0, None)[...].astype(F32) + a_mid[0].astype(F32) + a_mid[1].astype(F32)).astype(BF16)
    b_sum[...] = (b_piece(0, None)[...].astype(F32) + b_mid[0].astype(F32) + b_mid[1].astype(F32)).astype(BF16)

    quarter = half_rows // 2

    def a_next(i, part):
        rows = (pl.ds(0, half_rows), pl.ds(0, quarter), pl.ds(quarter, quarter))[0 if part is None else 1 + part]
        return a_sum.at[wrap(y + i), rows, :]

    def b_next(i, part):
        rows = (pl.ds(0, half_rows), pl.ds(0, quarter), pl.ds(quarter, quarter))[0 if part is None else 1 + part]
        return b_sum.at[rows, pl.ds(al(wrap(x + i) * BLK, 128), BLK)]

    sides = ((0, a_next, to_y), (1, b_next, to_x))
    for n, piece, to in sides:
        for s, part in signs:
            link.send((n, "raw2", s), piece(2, part), c_raw.at[n, part], to(s))
    for n, piece, to in sides:
        for s, part in signs:
            link.send((n, "own2", s), piece(s, 1 - part), c_mid.at[n, part, 1 - part], to(s))
    for n, piece, to in sides:
        for s, part in signs:
            link.arrived((n, "raw2", s), c_raw.at[n, part], to(-s))
            c_out[n, part] = (c_raw[n, part].astype(F32) + piece(s, part)[...].astype(F32)).astype(BF16)
            link.send((n, "sum2", s), c_out.at[n, part], c_mid.at[n, part, part], to(s))
    for n, piece, to in sides:
        for s, part in signs:
            link.arrived((n, "own2", s), c_mid.at[n, part, 1 - part], to(-s))
            link.arrived((n, "sum2", s), c_mid.at[n, part, part], to(-s))
        total = piece(0, None)[...].astype(F32)
        total = total + c_mid[n, 0].reshape(half_rows, BLK).astype(F32) + c_mid[n, 1].reshape(half_rows, BLK).astype(F32)
        out[pl.ds(al(y * RB + n * half_rows, 64), half_rows), own] = total.astype(BF16)

    def region(half, x, y, part):
        first, count = ((0, half_rows), (0, quarter), (quarter, quarter))[0 if part is None else 1 + part]
        return out.at[
            pl.ds(al(y * RB + half * half_rows + first, quarter), count),
            pl.ds(al(x * BLK, 128), BLK),
        ]

    all_gather_2d(link, region)
    link.drain()


def merger_sum(tokens, up, up_bias, src, down, text):
    vmem = pl.BlockSpec(memory_space=pltpu.VMEM)
    half_rows = RB // 2
    return pl.pallas_call(
        merger_kernel,
        out_shape=jax.ShapeDtypeStruct((TOK_SEQ, WIDTH), BF16),
        in_specs=[vmem] * 6,
        out_specs=vmem,
        scratch_shapes=[
            pltpu.VMEM((ROWS, HID), F32),
            pltpu.VMEM((TOK_SEQ, HID), BF16),
            pltpu.VMEM((SIDE, RB, WIDTH), BF16),
            pltpu.VMEM((2, 2, half_rows, BLK), BF16),
            pltpu.VMEM((2, SIDE, half_rows, BLK), BF16),
            pltpu.VMEM((2, 2, half_rows, BLK), BF16),
            pltpu.VMEM((SIDE, half_rows, BLK), BF16),
            pltpu.VMEM((2, half_rows, WIDTH // 2), BF16),
            pltpu.VMEM((2, half_rows, WIDTH), BF16),
            pltpu.VMEM((2, half_rows, WIDTH // 2), BF16),
            pltpu.VMEM((half_rows, WIDTH), BF16),
            pltpu.VMEM((2, 2, half_rows // 2, BLK), BF16),
            pltpu.VMEM((2, 2, 2, half_rows // 2, BLK), BF16),
            pltpu.VMEM((2, 2, half_rows // 2, BLK), BF16),
            pltpu.SemaphoreType.DMA((AG_SEMS + 24,)),
            pltpu.SemaphoreType.DMA((AG_SEMS + 24,)),
        ],
        compiler_params=pltpu.CompilerParams(collective_id=1, has_side_effects=True),
        name="merger",
    )(tokens, up, up_bias, src, down, text)


def kv_kernel(own, out, send_sem, recv_sem):
    s = lax.axis_index("seq")
    z, core = s // 2, lax.rem(s, 2)

    def at(dz, dc):
        return lax.rem(z + dz + SIDE, SIDE) * 2 + lax.rem(core + dc, 2)

    greet([at(1, 0), at(-1, 0), at(0, 1)], "seq")
    link = Link(send_sem, recv_sem, "seq")
    part_rows = TOK_SEQ // 2

    def reg(dz, dc, part):
        b = at(dz, dc)
        return out.at[b] if part is None else out.at[b, pl.ds(part * part_rows, part_rows)]

    signs = ((1, 0), (-1, 1))
    for sg, _ in signs:
        link.send(("z", sg), own, reg(0, 0, None), at(sg, 0))
    link.send(("c", 0), own, reg(0, 0, None), at(0, 1))
    out[s] = own[...]
    for sg, part in signs:
        link.arrived(("z", sg), reg(-sg, 0, None), at(-sg, 0))
        link.send(("r", sg), reg(-sg, 0, part), reg(-sg, 0, part), at(sg, 0))
        link.send(("c", -sg), reg(-sg, 0, None), reg(-sg, 0, None), at(0, 1))
    for sg, part in signs:
        link.arrived(("r", sg), reg(2, 0, part), at(-sg, 0))
        link.send(("c", 2, part), reg(2, 0, part), reg(2, 0, part), at(0, 1))
    for dz in (0, -1, 1):
        link.arrived(("c", dz), reg(dz, 1, None), at(0, 1))
    for part in (0, 1):
        link.arrived(("c", 2, part), reg(2, 1, part), at(0, 1))
    link.drain()


def gather_kv(own):
    vmem = pl.BlockSpec(memory_space=pltpu.VMEM)
    return pl.pallas_call(
        kv_kernel,
        out_shape=jax.ShapeDtypeStruct((N_SEQ, TOK_SEQ, 2 * HEAD_DIMENSION), BF16),
        in_specs=[vmem],
        out_specs=vmem,
        scratch_shapes=[pltpu.SemaphoreType.DMA((9,)), pltpu.SemaphoreType.DMA((9,))],
        compiler_params=pltpu.CompilerParams(collective_id=2, has_side_effects=True),
        name="kv",
    )(own)


def heads_kernel(own, out, send_sem, recv_sem):
    t, x, y = place()
    greet(ring_peers())
    link = Link(send_sem, recv_sem)
    out[:, pl.ds(al(t * HEAD_DIMENSION, 128), HEAD_DIMENSION)] = own[...]

    def region(half, x, y, part):
        first, count = ((0, 256), (0, 128), (128, 128))[0 if part is None else 1 + part]
        return out.at[pl.ds(half * 256 + first, count), pl.ds(al((x * SIDE + y) * HEAD_DIMENSION, 128), HEAD_DIMENSION)]

    all_gather_2d(link, region)
    link.drain()


def gather_heads(own):
    vmem = pl.BlockSpec(memory_space=pltpu.VMEM)
    return pl.pallas_call(
        heads_kernel,
        out_shape=jax.ShapeDtypeStruct((TOK_SEQ, LOCAL_QUERY_HEAD * HEAD_DIMENSION), BF16),
        in_specs=[vmem],
        out_specs=vmem,
        scratch_shapes=[pltpu.SemaphoreType.DMA((AG_SEMS,)), pltpu.SemaphoreType.DMA((AG_SEMS,))],
        compiler_params=pltpu.CompilerParams(collective_id=3, has_side_effects=True),
        name="heads",
    )(own)


def image_fields(image_table):
    grid_h = image_table[:, 0]
    grid_w = image_table[:, 1]
    across = grid_w // 2
    return (across, grid_h // 2 * across, image_table[:, 2])


def rope_tables(positions, across, counts, offsets, head_size):
    inside = (
        (positions[:, None] >= offsets[None, :]) & (positions[:, None] < (offsets + counts)[None, :])
    ).astype(jnp.int32)
    is_image = jnp.sum(inside, axis=1)
    run_start = jnp.sum(inside * offsets[None, :], axis=1)
    row_width = jnp.sum(inside * across[None, :], axis=1) + (1 - is_image)
    inner_index = positions - run_start
    pos_t = jnp.where(is_image > 0, run_start, positions)
    pos_h = jnp.where(is_image > 0, run_start + inner_index // row_width, positions)
    pos_w = jnp.where(is_image > 0, run_start + inner_index % row_width, positions)
    half_size = head_size // 2
    frequency = jnp.arange(half_size, dtype=jnp.int32)
    inverse = THETA ** (-2.0 * frequency.astype(F32) / head_size)
    first_cut = head_size // 8
    second_cut = first_cut + 3 * head_size // 16
    chosen = jnp.where(
        frequency[None, :] < first_cut,
        pos_t[:, None],
        jnp.where(frequency[None, :] < second_cut, pos_h[:, None], pos_w[:, None]),
    )
    angles = chosen.astype(F32) * inverse[None, :]
    angles = jnp.concatenate([angles, angles], axis=1)
    return (jnp.cos(angles), jnp.sin(angles), is_image)


def rotate(value, cosine, sine):
    half = value.shape[-1] // 2
    turned = jnp.concatenate([-value[:, half:], value[:, :half]], axis=-1)
    return value * cosine + turned * sine


def per_device(
    patches, image_table, ln_gain, ln_bias, merge_up, merge_up_bias, merge_down, merge_down_bias,
    text_embeds, attn_gain, q_weight, q_bias, key_value_weight, key_value_bias, o_weight,
):
    seq_index = lax.axis_index("seq")
    t = lax.axis_index("tp")
    positions = seq_index * TOK_SEQ + jnp.arange(TOK_SEQ, dtype=jnp.int32)
    begin = 2 * seq_index * N_TP
    group = lax.dynamic_slice_in_dim(image_table, begin, 2 * N_TP)
    across, counts, offsets = image_fields(group)
    cosine, sine, is_image = rope_tables(positions, across, counts, offsets, HEAD_DIMENSION)
    mask = is_image.astype(F32)
    starts = offsets.reshape(N_TP, 2)[:, 0]
    lengths = jnp.sum(counts.reshape(N_TP, 2), axis=1)
    devices = jnp.arange(N_TP, dtype=jnp.int32)
    base = jnp.sum(jnp.where(devices[None, :] < devices[:, None], lengths[None, :], 0), axis=1)
    k = jnp.arange(32, dtype=jnp.int32)
    mine = (devices == t).astype(jnp.int32)
    my_base, my_length = jnp.sum(mine * base), jnp.sum(mine * lengths)
    parity = jnp.arange(2, dtype=jnp.int32)
    token = 2 * k[None, :] + ((parity + my_base) % 2)[:, None]
    src_row = jnp.where(token < my_length, 4 * token, -8).reshape(CAP, 1)
    taken = 2 * k[None, :] + ((t + base) % 2)[:, None]
    target = jnp.where(taken < lengths[:, None], (base[:, None] + taken) // 2, -1).reshape(1, N_TP * 32)
    inner = positions[:, None] - starts[None, :]
    within = (inner >= 0) & (inner < lengths[None, :])
    compact = jnp.sum(jnp.where(within, base[None, :] + inner, 0), axis=1)
    src = jnp.where(is_image > 0, compact % 2 * 2 * HALF + compact // 2, -1).reshape(TOK_SEQ, 1)

    tokens = gather_tokens(patches, ln_gain.reshape(1, VW), ln_bias.reshape(1, VW), src_row, target)
    text = jnp.where(is_image[:, None] > 0, 0, text_embeds).astype(BF16)
    weight_cols = lax.all_to_all(
        o_weight, "tp", split_axis=1, concat_axis=0, tiled=True
    )
    summed = merger_sum(tokens, merge_up, merge_up_bias.reshape(1, HID), src, merge_down, text)
    residual = summed.astype(F32) + mask[:, None] * merge_down_bias[None, :]
    scale_rows = lax.rsqrt(jnp.mean(residual * residual, axis=1) + EPS)
    normed_rows = (residual * scale_rows[:, None] * attn_gain[None, :]).astype(BF16)

    kv_head = t * KEY_VALUE_HEADS // LOCAL_QUERY_HEAD
    key_at = kv_head * HEAD_DIMENSION
    value_at = KEY_VALUE_HEADS * HEAD_DIMENSION + key_at
    key_weight = lax.dynamic_slice_in_dim(key_value_weight, key_at, HEAD_DIMENSION, 1)
    value_weight = lax.dynamic_slice_in_dim(key_value_weight, value_at, HEAD_DIMENSION, 1)
    key_bias = lax.dynamic_slice_in_dim(key_value_bias, key_at, HEAD_DIMENSION)
    value_bias = lax.dynamic_slice_in_dim(key_value_bias, value_at, HEAD_DIMENSION)
    key = jnp.dot(normed_rows, key_weight, preferred_element_type=F32) + key_bias
    value = jnp.dot(normed_rows, value_weight, preferred_element_type=F32) + value_bias
    query = jnp.dot(normed_rows, q_weight, preferred_element_type=F32) + q_bias
    key = rotate(key, cosine, sine).astype(BF16)
    query = rotate(query, cosine, sine).astype(BF16)
    pieces = gather_kv(jnp.concatenate([key, value.astype(BF16)], axis=1))
    pieces = pieces.reshape(N_SEQ * TOK_SEQ, 2 * HEAD_DIMENSION)
    keys, values = pieces[:, :HEAD_DIMENSION], pieces[:, HEAD_DIMENSION:]
    key_position = jnp.arange(N_SEQ * TOK_SEQ, dtype=jnp.int32)
    scores = jnp.einsum("qd,kd->qk", query, keys, preferred_element_type=F32) * HEAD_DIMENSION ** (-0.5)
    allowed = key_position[None, :] <= positions[:, None]
    scores = jnp.where(allowed, scores, -1e30)
    best = jnp.max(scores, axis=1)
    weights = jnp.where(allowed, jnp.exp(scores - best[:, None]), 0.0)
    total = jnp.sum(weights, axis=1)
    acc = jnp.dot(weights.astype(BF16), values, preferred_element_type=F32)
    attention = (acc / total[:, None]).astype(BF16)
    gathered = gather_heads(attention)
    mixed = jnp.dot(gathered, weight_cols, preferred_element_type=F32)
    own_columns = lax.dynamic_slice_in_dim(summed, t * COLS, COLS, 1).astype(F32)
    own_bias = lax.dynamic_slice_in_dim(merge_down_bias, t * COLS, COLS)
    return (own_columns + mask[:, None] * own_bias[None, :] + mixed).astype(BF16)


def solution(mesh):
    return jax.shard_map(
        per_device,
        mesh=mesh,
        in_specs=(
            P(("seq", "tp"), None),
            P(),
            P(),
            P(),
            P(None, "tp"),
            P("tp"),
            P("tp", None),
            P(),
            P("seq", "tp"),
            P(),
            P(None, "tp"),
            P("tp"),
            P(),
            P(),
            P("tp", None),
        ),
        out_specs=P("seq", "tp"),
        check_vma=False,
    )
```

time: 356 us -> 213 us (0.60)
  waiting for transfers between devices: 216 us -> 0.01 us
  Pallas kernels: 0 us -> 147 us
  blocking collectives: 35.3 us -> 0 us
  between operations: 15.5 us -> 0.27 us
  matrix products: 34.1 us -> 19.3 us
  starting transfers between devices: 12.8 us -> 7.03 us
  local copies, waits for them, and re-layouts: 20.4 us -> 16.3 us
    pallas_call x0 -> x4, Pallas kernels: none -> 147 us  [the longest x1 61.7 us: merger_sum(): pl.pallas_call(merger_kernel, out_shape=jax.ShapeDtypeStruct((TOK_SEQ, WI...]
    psum x1 -> x0, waiting for transfers between devices: 130 us -> none  [per_device(): summed = lax.psum(term, 'tp')]
    all_gather x2 -> x0, waiting for transfers between devices: 64.6 us -> none  [the longest x1 51.1 us: per_device(): lax.all_gather(own_rows, 'tp', axis=0, tiled=True)]
    all_to_all x1 -> x0, blocking collectives: 35.3 us -> none  [copy_for_each(): lax.all_to_all(jnp.broadcast_to(shard[None], (peers, *shard.shape)), axis...]
    all_to_all x1 -> x0, waiting for transfers between devices: 20.6 us -> none  [per_device(): lax.all_to_all(outgoing, 'tp', split_axis=0, concat_axis=0, tiled=True)]
    dot_general x9 -> x6, matrix products: 34.1 us -> 19.3 us  [the longest x1 3.96 us: per_device(): jnp.einsum('qd,kd->qk', query, keys, preferred_element_type=F32)]
    all_to_all x1 -> x0, starting transfers between devices: 7.08 us -> none  [per_device(): lax.all_to_all(outgoing, 'tp', split_axis=0, concat_axis=0, tiled=True)]
    unnamed x24 -> x15, local copies, waits for them, and re-layouts: 4.24 us -> 9.32 us
  transfers between devices with their start and end apart: 5 -> 1, of which waited for: 4 -> 0; matrix products, arithmetic and copies ran while one was open for 5% -> 24% of each run, Pallas kernels for 0% -> 70%
where the time goes in v1:
time: 213 us; the launch traced here: 211 us
  Pallas kernels  147 us (69%)
  other arithmetic  20.1 us (9%)
  matrix products  19.3 us (9%)
  local copies, waits for them, and re-layouts  16.3 us (8%)
  starting transfers between devices  7.03 us (3%)
    pallas_call x1, Pallas kernels, merger_sum(): pl.pallas_call(merger_kernel, out_shape=jax.ShapeDtypeStruct((TOK_SEQ, WI...  61.7 us
    pallas_call x1, Pallas kernels, gather_tokens(): pl.pallas_call(tokens_kernel, out_shape=jax.ShapeDtypeStruct((ROWS, MW),...  47 us
    pallas_call x1, Pallas kernels, gather_heads(): pl.pallas_call(heads_kernel, out_shape=jax.ShapeDtypeStruct((TOK_SEQ, LOC...  21.7 us
    pallas_call x1, Pallas kernels, gather_kv(): pl.pallas_call(kv_kernel, out_shape=jax.ShapeDtypeStruct((N_SEQ, TOK_SEQ,...  17.1 us
    unnamed x15, local copies, waits for them, and re-layouts  9.32 us
    all_to_all x1, starting transfers between devices, per_device(): lax.all_to_all(o_weight, 'tp', split_axis=1, concat_axis=0, tiled=True)  7.03 us
    convert_element_type x1, other arithmetic, per_device(): (residual * scale_rows[:, None] * attn_gain[None, :]).astype(BF16)  5.83 us
  transfers between devices with their start and end apart: 1, of which 0 were waited for; matrix products, arithmetic and copies ran while one was open for 24% of the time, Pallas kernels for 70%

profile of v1, /device:TPU:96, one launch (start us, length us, event | category | flops | bytes accessed | tf_op | source)
XLA Modules:
  0.0 210.6 jit_solution(5394316740283484902)
XLA Ops:
  0.0 0.0 copy-start
  0.0 0.0 copy-start.4
  0.0 2.3 %copy.65 = bf16[128,3584]{0,1:T(8,128)(2,1)} copy(bf16[128,3584]{1,0:T(8,128)(2,1)} %param.29) | data formatting | bytes 1835008 | tf_op args[14]
  2.3 7.0 %all-to-all-start = ((bf16[128,16,224]{0,2,1:T(8,128)(2,1)}), bf16[128,16,224]{0,2,1:T(8,128)(2,1)S(1)}, u32[]{:S(2)}, u32[]{:S(2)}) async-start(bf16[128,16,224]{0,2,1:T(8,128)(2,1)} %bitcast.5), calls=%async_computation | async-start | bytes 1835008 | tf_op jit(solution)/shard_map/all_to_all | solution.py:512
  9.4 0.8 constant_dynamic-slice_fusion
  10.2 0.1 squeeze.11
  10.3 0.1 squeeze.12
  10.3 0.1 fusion.39
  10.5 0.1 select_reduce_fusion.2
  10.6 0.7 and_select_fusion.3
  11.3 0.1 add_add_fusion
  11.4 0.1 add_compare_fusion
  11.5 0.1 add.315
  11.6 0.1 lt.145
  11.7 0.7 and_select_fusion.4
  12.4 0.8 compare_select_fusion.8
  13.1 0.7 select_n.249.src_row
  13.9 1.3 reshape.439.gain
  15.1 1.3 reshape.440.bias
  16.4 0.1 reshape_squeeze.3
  16.5 0.1 slice_reduce_fusion
  16.6 0.1 fusion.35
  16.7 0.2 copy.55
  16.9 1.1 copy.60
  18.0 0.1 select_reduce_fusion
  18.1 1.0 fusion.22.src
  19.1 0.8 broadcast_select_fusion.text
  19.9 5.9 %copy.61.up = bf16[5120,320]{1,0:T(8,128)(2,1)} copy(bf16[5120,320]{0,1:T(8,128)(2,1)} %param.19) | data formatting | bytes 6553600 | tf_op args[4]
  25.8 0.0 copy-done.4
  25.8 0.5 reshape.441.up_bias
  26.4 0.1 fusion.44
  26.5 0.6 fusion.49.target
  27.1 47.0 %tokens.1 = bf16[448,5120]{1,0:T(8,128)(2,1)} custom-call(bf16[256,1280]{1,0:T(8,128)(2,1)} %patches.1, f32[1,1280]{1,0:T(1,128)} %reshape.439.gain, f32[1,1280]{1,0:T(1,128)} %reshape.440.bias, s32[64,1]{1,0:T(8,128)} %select_n.249.src_row, s32[1,512]{1,0:T(1,128)} %fusion.49.target), custom_call_target="tpu_custom_call" | custom-call | tf_op jit(solution)/shard_map/tokens/pallas_call | solution.py:203
  74.1 0.0 copy-start.2
  74.1 0.0 copy-start.3
  74.1 61.7 %merger.1 = bf16[512,3584]{1,0:T(8,128)(2,1)} custom-call(bf16[448,5120]{1,0:T(8,128)(2,1)} %tokens.1, bf16[5120,320]{1,0:T(8,128)(2,1)} %copy.61.up, f32[1,320]{1,0:T(1,128)} %reshape.441.up_bias, s32[512,1]{1,0:T(8,128)} %fusion.22.src, bf16[320,3584]{1,0:T(8,128)(2,1)} %down.1, bf16[512,224]{1,0:T(8,128)(2,1)} %broadcast_select_fusion.text), custom_call_target="tpu_custom_call" | custom-call | tf_op jit(solution)/shard_map/merger/pallas_call | solution.py:340
  135.8 0.0 copy-done.2
  135.9 3.4 %multiply_reduce_fusion = f32[512]{0:T(512)S(1)} fusion(bf16[512,3584]{1,0:T(8,128)(2,1)} %merger.1, f32[3584]{0:T(1024)S(1)} %copy-done.2, f32[512]{0:T(512)S(1)} %get-tuple-element.23), kind=kLoop, calls=%fused_computation.4 | loop fusion | flops 9174528 | bytes 3688448 | tf_op jit(solution)/shard_map/reduce_sum | solution.py:517
  139.2 0.0 copy-done.3
  139.3 5.8 %multiply_convert_fusion = bf16[512,3584]{1,0:T(8,128)(2,1)} fusion(bf16[512,3584]{1,0:T(8,128)(2,1)} %merger.1, f32[3584]{0:T(1024)S(1)} %copy-done.3, f32[512]{0:T(512)S(1)} %add_rsqrt_fusion, f32[3584]{0:T(1024)S(1)} %copy-done.2, f32[512]{0:T(512)S(1)} %get-tuple-element.23), kind=kLoop, calls=%fused_computation.3 | loop fusion | flops 11010048 | bytes 7372800 | tf_op jit(solution)/shard_map/convert_element_type | solution.py:518
  145.1 0.8 fusion.63
  145.9 0.0 copy-start.5
  145.9 3.5 %convolution_add_fusion.2 = f32[512,128]{1,0:T(8,128)S(1)} fusion(bf16[512,3584]{1,0:T(8,128)(2,1)} %multiply_convert_fusion, bf16[3584,1024]{1,0:T(8,128)(2,1)} %param.27, s32[]{:T(128)S(6)} %select_n.245, f32[128]{0:T(128)S(1)} %get-tuple-element.21), kind=kOutput, calls=%fused_computation.13 | convolution fusion | flops 469827584 | bytes 4850180 | tf_op jit(solution)/shard_map/dot_general | solution.py:527
  149.4 0.1 slice_negate_fusion
  149.5 3.4 %fusion.6 = bf16[512,128]{1,0:T(8,128)(2,1)S(1)} fusion(bf16[512,3584]{1,0:T(8,128)(2,1)} %multiply_convert_fusion, bf16[3584,1024]{1,0:T(8,128)(2,1)} %param.27, s32[]{:T(128)S(6)} %select_n.246, f32[128]{0:T(128)S(1)} %get-tuple-element.22), kind=kOutput, calls=%fused_computation.15 | convolution fusion | flops 469893120 | bytes 4719108 | tf_op jit(solution)/shard_map/dot_general | solution.py:528
  152.9 0.3 convert_multiply_fusion
  153.2 1.4 fusion.26
  154.6 0.7 pad_maximum_fusion.1.own
  155.4 17.1 %kv.1 = bf16[8,512,256]{2,1,0:T(8,128)(2,1)} custom-call(bf16[512,256]{1,0:T(8,128)(2,1)} %pad_maximum_fusion.1.own), custom_call_target="tpu_custom_call" | custom-call | tf_op jit(solution)/shard_map/kv/pallas_call | solution.py:404
  172.4 0.0 copy-done
  172.5 0.0 copy-done.5
  172.5 3.2 %convolution_add_fusion.3 = f32[512,128]{1,0:T(8,128)S(1)} fusion(bf16[512,3584]{1,0:T(8,128)(2,1)} %multiply_convert_fusion, bf16[3584,128]{1,0:T(8,128)(2,1)S(1)} %copy-done, f32[128]{0:T(128)S(1)} %copy-done.5), kind=kOutput, calls=%fused_computation.14 | convolution fusion | flops 469827584 | bytes 4850176 | tf_op jit(solution)/shard_map/dot_general | solution.py:529
  175.7 0.1 slice_negate_fusion.1
  175.8 4.0 %fusion = (f32[512]{0:T(512)S(1)}, f32[512,4096]{1,0:T(8,128)S(1)}) fusion(s32[512]{0:T(512)S(1)} %iota_add_fusion, bf16[4096,256]{1,0:T(8,128)(2,1)} %bitcast.39, f32[512,64]{1,0:T(8,128)S(1)} %get-tuple-element.16, f32[512,64]{1,0:T(8,128)S(1)} %get-tuple-element.15, f32[512,128]{1,0:T(8,128)S(1)} %convolution_add_fusion.3, ...), kind=kOutput, calls=%fused_computation.6 | convolution fusion | flops 545652224 | bytes 10096640 | tf_op jit(solution)/shard_map/qd,kd->qk/dot_general | solution.py:536
  179.8 0.0 copy-start.1
  179.8 2.8 %fusion.1 = f32[512]{0:T(512)S(1)} fusion(f32[512,4096]{1,0:T(8,128)S(1)} %get-tuple-element.28, f32[512]{0:T(512)S(1)} %get-tuple-element.27, s32[512]{0:T(512)S(1)} %iota_add_fusion), kind=kLoop, calls=%fused_computation.7 | loop fusion | flops 12582400 | bytes 8394752 | tf_op jit(solution)/shard_map/reduce_sum | solution.py:541
  182.6 0.0 copy-done.1
  182.6 3.0 %fusion.10.own = bf16[512,128]{1,0:T(8,128)(2,1)} fusion(f32[512,4096]{1,0:T(8,128)S(1)} %get-tuple-element.28, f32[512]{0:T(512)S(1)} %get-tuple-element.27, s32[512]{0:T(512)S(1)} %iota_add_fusion, bf16[4096,256]{1,0:T(8,128)(2,1)S(1)} %bitcast.40, f32[512]{0:T(512)S(1)} %fusion.1), kind=kOutput, calls=%fused_computation.17 | convolution fusion | flops 549584896 | bytes 9574400 | tf_op jit(solution)/shard_map/dot_general | solution.py:542
  185.6 21.7 %heads.1 = bf16[512,2048]{1,0:T(8,128)(2,1)} custom-call(bf16[512,128]{1,0:T(8,128)(2,1)} %fusion.10.own), custom_call_target="tpu_custom_call" | custom-call | tf_op jit(solution)/shard_map/heads/pallas_call | solution.py:431
  207.3 0.1 dynamic_slice.23
  207.4 0.0 all-to-all-done
  207.4 2.4 %fusion.5 = bf16[512,224]{1,0:T(8,128)(2,1)S(1)} fusion(bf16[512,2048]{1,0:T(8,128)(2,1)} %heads.1, f32[224]{0:T(256)S(1)} %dynamic_slice.23, f32[512]{0:T(512)S(1)} %get-tuple-element.23, bf16[512,3584]{1,0:T(8,128)(2,1)} %merger.1, s32[]{:T(128)S(6)} %select_n.235, bf16[128,16,224]{0,2,1:T(8,128)(2,1)S(1)} %all-to-all-done), kind=kOutput, calls=%fused_computation.11 | convolution fusion | flops 470335488 | bytes 3476356 | tf_op jit(solution)/shard_map/dot_general | solution.py:545
  209.7 0.8 copy.68
  (8 shorter events, 0.1 us)
Async XLA Ops:
  0.0 172.4 %copy-start = (bf16[3584,128]{1,0:T(8,128)(2,1)S(1)}, bf16[3584,128]{1,0:T(8,128)(2,1)}, u32[]{:S(2)}) copy-start(bf16[3584,128]{1,0:T(8,128)(2,1)} %param.25) | copy-start | bytes 2752516
  0.0 25.8 %copy-start.4 = (f32[320]{0:T(512)S(1)}, f32[320]{0:T(512)}, u32[]{:S(2)}) copy-start(f32[320]{0:T(512)} %param.20) | copy-start | bytes 3844
  2.3 205.0 %all-to-all-start = ((bf16[128,16,224]{0,2,1:T(8,128)(2,1)}), bf16[128,16,224]{0,2,1:T(8,128)(2,1)S(1)}, u32[]{:S(2)}, u32[]{:S(2)}) async-start(bf16[128,16,224]{0,2,1:T(8,128)(2,1)} %bitcast.5), calls=%async_computation | async-start | bytes 1835008 | tf_op jit(solution)/shard_map/all_to_all | solution.py:512
  74.1 61.7 %copy-start.2 = (f32[3584]{0:T(1024)S(1)}, f32[3584]{0:T(1024)}, u32[]{:S(2)}) copy-start(f32[3584]{0:T(1024)} %param.22) | copy-start | bytes 43012
  74.1 65.1 %copy-start.3 = (f32[3584]{0:T(1024)S(1)}, f32[3584]{0:T(1024)}, u32[]{:S(2)}) copy-start(f32[3584]{0:T(1024)} %param.24) | copy-start | bytes 43012
  145.9 26.5 %copy-start.5 = (f32[128]{0:T(128)S(1)}, f32[128]{0:T(128)}, u32[]{:S(2)}) copy-start(f32[128]{0:T(128)} %param.26) | copy-start | bytes 1540
  179.8 2.9 %copy-start.1 = (bf16[8,512,256]{2,1,0:T(8,128)(2,1)S(1)}, bf16[8,512,256]{2,1,0:T(8,128)(2,1)}, u32[]{:S(2)}) copy-start(bf16[8,512,256]{2,1,0:T(8,128)(2,1)} %kv.1) | copy-start | bytes 6291460

commit v2 on v1

v2 whole, which is shorter than its diff:
```python
import functools

import jax
import jax.numpy as jnp
from jax import lax
from jax.experimental import pallas as pl
from jax.experimental.pallas import tpu as pltpu
from jax.sharding import PartitionSpec as P

MESH = pl.DeviceIdType.MESH
HEAD_DIMENSION = 128
KEY_VALUE_HEADS = 4
LOCAL_QUERY_HEAD = 16
CAP = 64
TOK_SEQ = 512
MW = 5120
VW = 1280
WIDTH = 3584
HID = 320
COLS = 224
N_TP = 16
N_SEQ = 8
SIDE = 4
ROWS = 448
HALF = 112
TCOL = 640
BLK = 896
RB = 128

EPS = 1e-06
THETA = 1000000.0
F32 = jnp.float32
BF16 = jnp.bfloat16


def al(value, multiple):
    return pl.multiple_of(value, multiple)


def place():
    t = lax.axis_index("tp")
    return t, t // SIDE, lax.rem(t, SIDE)


def wrap(value):
    return lax.rem(value + 2 * SIDE, SIDE)


def at_xy(x, y):
    return wrap(x) * SIDE + wrap(y)


def offset_xy(half, i, j):
    t, x, y = place()
    return (wrap(x + j), wrap(y + i)) if half == 0 else (wrap(x + i), wrap(y + j))


def peer(half, phase, sign):
    x, y = offset_xy(half, sign, 0) if phase == 1 else offset_xy(half, 0, sign)
    return x * SIDE + y


class Link:
    def __init__(self, send_sem, recv_sem, axis="tp"):
        self.send_sem, self.recv_sem, self.axis = send_sem, recv_sem, axis
        self.number, self.open = {}, []

    def _copy(self, key, src, dst, device):
        k = self.number.setdefault(key, len(self.number))
        return pltpu.make_async_remote_copy(
            src_ref=src,
            dst_ref=dst,
            send_sem=self.send_sem.at[k],
            recv_sem=self.recv_sem.at[k],
            device_id={self.axis: device},
            device_id_type=MESH,
        )

    def send(self, key, src, dst, device):
        copy = self._copy(key, src, dst, device)
        copy.start()
        self.open.append(copy)

    def arrived(self, key, dst, device):
        self._copy(key, dst, dst, device).wait_recv()

    def drain(self):
        assert len(self.number) <= self.send_sem.shape[0]
        for copy in self.open:
            copy.wait_send()
        self.open = []


def all_gather_2d(link, region, tag, own=None, hooks=(), lead=0):
    def reg(half, i, j, part):
        x, y = offset_xy(half, i, j)
        return region(half, x, y, part)

    def send(key, half, phase, sign, i, j, part):
        ref = reg(half, i, j, part)
        src = own(half) if own is not None and i == 0 and j == 0 else ref
        link.send((tag, half, *key), src, ref, peer(half, phase, sign))

    def got(key, half, phase, sign, i, j, part):
        link.arrived((tag, half, *key), reg(half, i, j, part), peer(half, phase, -sign))

    both = ((1, 0), (-1, 1))
    halves = (0, 1)

    def last(i, h):
        for s, part in both:
            got(("r2", s, i), h, 2, s, i, 2, part)

    for h in halves:
        for s, _ in both:
            send(("p1", s), h, 1, s, 0, 0, None)
    for h in halves:
        for s, _ in both:
            send(("p2", s, 0), h, 2, s, 0, 0, None)
    for s, part in both:
        for h in halves:
            got(("p1", s), h, 1, s, -s, 0, None)
            send(("r1", s), h, 1, s, -s, 0, part)
            for s2, _ in both:
                send(("p2", s2, -s), h, 2, s2, -s, 0, None)
    for s, part in both:
        for h in halves:
            got(("p2", s, 0), h, 2, s, 0, -s, None)
            send(("r2", s, 0), h, 2, s, 0, -s, part)
    for s, part in both:
        for h in halves:
            got(("r1", s), h, 1, s, 2, 0, part)
            for s2, _ in both:
                send(("p2", s2, 2, part), h, 2, s2, 2, 0, part)
    for i in (-1, 1):
        for s, part in both:
            for h in halves:
                got(("p2", s, i), h, 2, s, i, -s, None)
                send(("r2", s, i), h, 2, s, i, -s, part)
    last(0, lead)
    if hooks:
        hooks[0]()
    for s, part in both:
        for h in halves:
            got(("p2", s, 2, part), h, 2, s, 2, -s, part)
            send(("r2", s, 2), h, 2, s, 2, -s, part)
    for s, part in both:
        for h in halves:
            got(("p2", s, 2, 1 - part), h, 2, s, 2, -s, 1 - part)
    for n, i in enumerate((-1, 1)):
        last(i, lead)
        if hooks:
            hooks[1 + n]()
    last(2, lead)
    for i in (0, -1, 1, 2):
        last(i, 1 - lead)
    if hooks:
        hooks[3]()


AG_SEMS = 44


ORDER = (0, -1, 1, 2)
SIGNS = ((1, 0), (-1, 1))
HROW = RB // 2
QROW = RB // 4
D = HEAD_DIMENSION


def chosen(index, pieces):
    value = pieces[0]
    for k in range(1, len(pieces)):
        value = jnp.where(index == k, pieces[k], value)
    return value


def row_of(ref):
    return ref[...].reshape(1, ref.shape[0])


def layout(table, s):
    start, length, base = [], [], []
    so_far = 0
    for e in range(N_TP):
        i = 2 * N_TP * s + 2 * e
        first = (table[0, i] // 2) * (table[1, i] // 2)
        second = (table[0, i + 1] // 2) * (table[1, i + 1] // 2)
        start.append(table[2, i])
        length.append(first + second)
        base.append(so_far)
        so_far = so_far + first + second
    return start, length, base


def body(
    table, patches, ln_gain, ln_bias, up_hbm, up_bias, down_hbm, down_bias, text, gain, q_weight, q_bias,
    kv_weight, kv_bias, o_hbm, cosine, sine, out,
    up, down, o_rows, o_send, o_cols, outgoing, incoming, tokens, lifted, hidden, pa, pb,
    a_raw, a_mid, a_out, a_sum, b_raw, b_mid, b_out, b_sum, c_raw, c_mid, c_out, shard,
    rows_ref, weight, normed, query, kv, heads, best, total, acc, load_sem, send_sem, recv_sem, seq_send, seq_recv,
):
    t, x, y = place()
    s = lax.axis_index("seq")
    z, core = s // 2, lax.rem(s, 2)

    def at(dz, dc):
        return lax.rem(z + dz + SIDE, SIDE) * 2 + lax.rem(core + dc, 2)

    barrier = pltpu.get_barrier_semaphore()
    for o in range(1, N_TP):
        pl.semaphore_signal(barrier, inc=1, device_id={"tp": lax.rem(t + o, N_TP)}, device_id_type=MESH)
    for device in (at(1, 0), at(-1, 0), at(0, 1)):
        pl.semaphore_signal(barrier, inc=1, device_id={"seq": device}, device_id_type=MESH)

    def load(n, src, dst):
        copy = pltpu.make_async_copy(src, dst, load_sem.at[n])
        copy.start()
        return copy

    load_o = load(0, o_hbm.at[pl.ds(al(s * 16, 16), 16), :], o_rows)
    load_up = load(1, up_hbm, up)
    load_down = load(2, down_hbm, down)
    load_qkv = [
        load(3, q_weight, weight.at[:, pl.ds(0, D)]),
        load(4, kv_weight.at[:, pl.ds(al(x * D, 128), D)], weight.at[:, pl.ds(D, D)]),
        load(5, kv_weight.at[:, pl.ds(al((KEY_VALUE_HEADS + x) * D, 128), D)], weight.at[:, pl.ds(2 * D, D)]),
    ]
    link = Link(send_sem, recv_sem)
    along = Link(seq_send, seq_recv, "seq")
    start, length, base = layout(table, s)

    value = patches[...].astype(F32)
    centre = jnp.mean(value, axis=-1, keepdims=True)
    centred = value - centre
    spread = jnp.mean(centred * centred, axis=-1, keepdims=True)
    fine = (centred * lax.rsqrt(spread + EPS) * row_of(ln_gain) + row_of(ln_bias)).astype(BF16)
    my_base, my_length = chosen(t, base), chosen(t, length)
    slot = lax.broadcasted_iota(jnp.int32, (CAP, 4 * CAP), 0)
    lane = lax.broadcasted_iota(jnp.int32, (CAP, 4 * CAP), 1)
    token = 2 * lax.rem(slot, 32) + lax.rem(slot // 32 + my_base, 2)
    source = jnp.where(token < my_length, 4 * token, -8)
    pl.semaphore_wait(barrier, N_TP + 2)
    for i in (1, 2, 3, 0):
        q = wrap(x + i)
        part = jnp.dot((lane == source + q).astype(BF16), fine, preferred_element_type=F32).astype(BF16)
        for u in range(2):
            for r in range(2):
                outgoing[4 * q + 2 * u + r] = part[r * 32 : (r + 1) * 32, u * TCOL : (u + 1) * TCOL]
        for j in (1, 2, 3, 0):
            if (i, j) != (0, 0):
                to = at_xy(x + i, y + j)
                link.send(("a", i, j), outgoing.at[to], incoming.at[t], to)
    incoming[t] = outgoing[t]

    load_o.wait()
    o_all = o_rows[...]
    for d in range(N_TP):
        o_send[d] = o_all[:, d * COLS : (d + 1) * COLS]
    o_place = pl.ds(al(s * 16, 16), 16)
    for o in range(1, N_TP):
        to = lax.rem(t + o, N_TP)
        link.send(("o", o), o_send.at[to], o_cols.at[t, o_place, :], to)
    o_cols[t, o_place, :] = o_send[t]

    half_of = lax.rem(t, 2)
    lane = lax.broadcasted_iota(jnp.int32, (1, N_TP * 32), 1)
    base_row = jnp.zeros((1, N_TP * 32), jnp.int32)
    length_row = base_row
    for e in range(N_TP):
        here = lane // 32 == e
        base_row = jnp.where(here, base[e], base_row)
        length_row = jnp.where(here, length[e], length_row)
    taken = 2 * lax.rem(lane, 32) + lax.rem(half_of + base_row, 2)
    target = jnp.where(taken < length_row, (base_row + taken) // 2, -1)
    pick = (lax.broadcasted_iota(jnp.int32, (2 * HALF, N_TP * 32), 0) == target).astype(BF16)
    for i in (1, 2, 3, 0):
        for j in (1, 2, 3, 0):
            if (i, j) != (0, 0):
                frm = at_xy(x - i, y - j)
                link.arrived(("a", i, j), incoming.at[frm], frm)
    slots = incoming[...].reshape(N_TP * 32, TCOL)
    mine = jnp.dot(pick, slots, preferred_element_type=F32).astype(BF16)
    tokens[pl.ds(al(half_of * 2 * HALF, 2 * HALF), 2 * HALF), pl.ds(al(t // 2 * TCOL, 128), TCOL)] = mine

    def token_region(half, x, y, part):
        d = x * SIDE + y
        first, width = ((0, TCOL), (0, 384), (384, 256))[0 if part is None else 1 + part]
        return tokens.at[
            pl.ds(al(lax.rem(d, 2) * 2 * HALF + half * HALF, 16), HALF),
            pl.ds(al(d // 2 * TCOL + first, 128), width),
        ]

    def o_region(dz, dc, part):
        first, count = ((0, N_TP), (0, 8), (8, 8))[0 if part is None else 1 + part]
        return o_cols.at[pl.ds(first, count), pl.ds(al(at(dz, dc) * 16, 16), 16), :]

    def lift(n):
        cols = pl.ds(al(wrap(x + ORDER[n]) * VW, 128), VW)
        got = lax.dot_general(
            tokens[:, cols], up[:, cols], (((1,), (1,)), ((), ())), preferred_element_type=F32
        )
        if n == 0:
            lifted[...] = got + row_of(up_bias)
        else:
            lifted[...] += got

    def lift_first():
        load_up.wait()
        lift(0)
        for o in range(1, N_TP):
            frm = lax.rem(t - o + N_TP, N_TP)
            link.arrived(("o", o), o_cols.at[frm, o_place, :], frm)
        for sg, _ in SIGNS:
            along.send(("o", "z", sg), o_region(0, 0, None), o_region(0, 0, None), at(sg, 0))
        along.send(("o", "c", 0), o_region(0, 0, None), o_region(0, 0, None), at(0, 1))

    all_gather_2d(
        link, token_region, "t", None,
        (lift_first, functools.partial(lift, 1), functools.partial(lift, 2), functools.partial(lift, 3)), 1,
    )

    raised = lifted[...]
    act = (0.5 * raised * (1.0 + lax.erf(raised * 0.5**0.5))).astype(BF16)
    order = lax.broadcasted_iota(jnp.int32, (TOK_SEQ, 1), 0)
    pos = s * TOK_SEQ + lax.rem(order, 256) // HROW * RB + order // 256 * HROW + lax.rem(order, HROW)
    where = jnp.full((TOK_SEQ, 1), -1, jnp.int32)
    for e in range(N_TP):
        inner = pos - start[e]
        where = jnp.where((inner >= 0) & (inner < length[e]), base[e] + inner, where)
    where = jnp.where(where >= 0, lax.rem(where, 2) * 2 * HALF + where // 2, -1)
    pick = (lax.broadcasted_iota(jnp.int32, (TOK_SEQ, ROWS), 1) == where).astype(BF16)
    hidden[...] = jnp.dot(pick, act, preferred_element_type=F32).astype(BF16)
    load_down.wait()
    spot = (
        lax.broadcasted_iota(jnp.int32, (COLS, BLK), 0) + y * COLS == lax.broadcasted_iota(jnp.int32, (COLS, BLK), 1)
    ).astype(BF16)
    own = pl.ds(al(x * BLK, 128), BLK)
    at_lane = s * TOK_SEQ + lax.broadcasted_iota(jnp.int32, (1, TOK_SEQ), 1)
    plain = jnp.ones((1, TOK_SEQ), F32)
    for e in range(N_TP):
        plain = jnp.where((at_lane >= start[e]) & (at_lane < start[e] + length[e]), 0.0, plain)
    words = (text[...].astype(F32) * plain).astype(BF16)

    def words_of(rb):
        return lax.dot_general(
            words[:, rb * RB : (rb + 1) * RB], spot, (((0,), (0,)), ((), ())), preferred_element_type=F32
        )

    def lower_a(i):
        cols = pl.ds(al(wrap(x + i) * BLK, 128), BLK)
        got = jnp.dot(hidden[0:256, :], down[:, cols], preferred_element_type=F32)
        pa[:, :, cols] = got.astype(BF16).reshape(SIDE, HROW, BLK)

    def lower_b(i):
        rb = wrap(y + i)
        got = jnp.dot(hidden[pl.ds(al(256 + rb * HROW, HROW), HROW), :], down[...], preferred_element_type=F32)
        pb[rb] = got.astype(BF16)

    for rb in range(SIDE):
        add = words_of(rb)
        a_add = add[:HROW]
        pb_add = add[HROW:]
        a_sum[rb] = a_add.astype(BF16)
        b_words = pb_add.astype(BF16)
        b_sum[pl.ds(0, HROW), pl.ds(rb * BLK, BLK)] = b_words

    def a_piece(i, part):
        rows = (pl.ds(0, SIDE), pl.ds(0, 2), pl.ds(2, 2))[0 if part is None else 1 + part]
        return pa.at[rows, :, pl.ds(al(wrap(x + i) * BLK, 128), BLK)]

    def b_piece(i, part):
        cols = (pl.ds(0, WIDTH), pl.ds(0, WIDTH // 2), pl.ds(WIDTH // 2, WIDTH // 2))[0 if part is None else 1 + part]
        return pb.at[wrap(y + i), :, cols]

    def to_x(sg):
        return at_xy(x + sg, y)

    def to_y(sg):
        return at_xy(x, y + sg)

    def mid_of(ref, name, part):
        if name == "a":
            return ref.at[pl.ds(2 * part, 2)]
        return ref.at[:, pl.ds(part * (WIDTH // 2), WIDTH // 2)]

    def make_a(i):
        lower_a(i)
        if i == 0:
            pa[:, :, own] = (pa[:, :, own].astype(F32) + a_sum[...].astype(F32)).astype(BF16)

    def make_b(i):
        lower_b(i)
        rb = wrap(y + i)
        add = b_sum[:, pl.ds(al(rb * BLK, 128), BLK)].astype(F32)
        pb[rb, :, own] = (pb[rb, :, own].astype(F32) + add).astype(BF16)

    sides = (
        ("a", a_piece, a_raw, a_mid, a_out, to_x, make_a),
        ("b", b_piece, b_raw, b_mid, b_out, to_y, make_b),
    )
    for n, piece, raw, mid, outb, to, make in sides:
        make(2)
        for sg, part in SIGNS:
            link.send((n, "raw", sg), piece(2, part), raw.at[part], to(sg))
    for sg, part in SIGNS:
        for n, piece, raw, mid, outb, to, make in sides:
            make(sg)
            link.send((n, "own", sg), piece(sg, 1 - part), mid_of(mid.at[part], n, 1 - part), to(sg))
    for n, piece, raw, mid, outb, to, make in sides:
        for sg, part in SIGNS:
            link.arrived((n, "raw", sg), raw.at[part], to(-sg))
            outb[part] = (raw[part].astype(F32) + piece(sg, part)[...].astype(F32)).astype(BF16)
            link.send((n, "sum", sg), outb.at[part], mid_of(mid.at[part], n, part), to(sg))
    for n, piece, raw, mid, outb, to, make in sides:
        make(0)

    for sg, part in SIGNS:
        along.arrived(("o", "z", sg), o_region(-sg, 0, None), at(-sg, 0))
        along.send(("o", "r", sg), o_region(-sg, 0, part), o_region(-sg, 0, part), at(sg, 0))
        along.send(("o", "c", -sg), o_region(-sg, 0, None), o_region(-sg, 0, None), at(0, 1))

    def a_next(i, part):
        rows = (pl.ds(0, HROW), pl.ds(0, QROW), pl.ds(QROW, QROW))[0 if part is None else 1 + part]
        return a_sum.at[wrap(y + i), rows, :]

    def b_next(i, part):
        rows = (pl.ds(0, HROW), pl.ds(0, QROW), pl.ds(QROW, QROW))[0 if part is None else 1 + part]
        return b_sum.at[rows, pl.ds(al(wrap(x + i) * BLK, 128), BLK)]

    after = ((0, a_next, to_y), (1, b_next, to_x))
    for side, nxt in zip(sides, after):
        n, piece, raw, mid, outb, to, make = side
        for sg, part in SIGNS:
            link.arrived((n, "own", sg), mid_of(mid.at[part], n, 1 - part), to(-sg))
            link.arrived((n, "sum", sg), mid_of(mid.at[part], n, part), to(-sg))
        held = a_sum if n == "a" else b_sum
        held[...] = (piece(0, None)[...].astype(F32) + mid[0].astype(F32) + mid[1].astype(F32)).astype(BF16)
        n, piece, to = nxt
        for sg, part in SIGNS:
            link.send((n, "raw2", sg), piece(2, part), c_raw.at[n, part], to(sg))
        for sg, part in SIGNS:
            link.send((n, "own2", sg), piece(sg, 1 - part), c_mid.at[n, part, 1 - part], to(sg))
    for n, piece, to in after:
        for sg, part in SIGNS:
            link.arrived((n, "raw2", sg), c_raw.at[n, part], to(-sg))
            c_out[n, part] = (c_raw[n, part].astype(F32) + piece(sg, part)[...].astype(F32)).astype(BF16)
            link.send((n, "sum2", sg), c_out.at[n, part], c_mid.at[n, part, part], to(sg))
    row = s * TOK_SEQ + y * RB + lax.broadcasted_iota(jnp.int32, (RB, 1), 0)
    image = jnp.zeros((RB, 1), F32)
    for e in range(N_TP):
        image = jnp.where((row >= start[e]) & (row < start[e] + length[e]), 1.0, image)
    full_bias = row_of(down_bias)
    shift = image * chosen(x, [full_bias[:, k * BLK : (k + 1) * BLK] for k in range(SIDE)])
    for n, piece, to in after:
        for sg, part in SIGNS:
            link.arrived((n, "own2", sg), c_mid.at[n, part, 1 - part], to(-sg))
            link.arrived((n, "sum2", sg), c_mid.at[n, part, part], to(-sg))
        held = piece(0, None)[...].astype(F32)
        held = held + c_mid[n, 0].reshape(HROW, BLK).astype(F32) + c_mid[n, 1].reshape(HROW, BLK).astype(F32)
        shard[pl.ds(n * HROW, HROW), :] = (held + shift[n * HROW : (n + 1) * HROW]).astype(BF16)

    for sg, part in SIGNS:
        along.arrived(("o", "r", sg), o_region(2, 0, part), at(-sg, 0))
        along.send(("o", "c", 2, part), o_region(2, 0, part), o_region(2, 0, part), at(0, 1))

    def region(half, x, y, part):
        first, count = ((0, HROW), (0, QROW), (QROW, QROW))[0 if part is None else 1 + part]
        return rows_ref.at[
            pl.ds(al(y * RB + half * HROW + first, QROW), count),
            pl.ds(al(x * BLK, 128), BLK),
        ]

    def kv_at(n, dz, dc, part):
        first, count = ((0, RB), (0, HROW), (HROW, HROW))[0 if part is None else 1 + part]
        return kv.at[at(dz, dc), pl.ds(al(wrap(y + ORDER[n]) * RB + first, HROW), count), :]

    kv_row = row_of(kv_bias)
    heads_of = [kv_row[:, k * D : (k + 1) * D] for k in range(2 * KEY_VALUE_HEADS)]
    key_bias, value_bias = chosen(x, heads_of[:KEY_VALUE_HEADS]), chosen(x, heads_of[KEY_VALUE_HEADS:])

    def project(n):
        rows = pl.ds(al(wrap(y + ORDER[n]) * RB, RB), RB)
        value = rows_ref[rows, :].astype(F32)
        scale = lax.rsqrt(jnp.mean(value * value, axis=-1, keepdims=True) + EPS)
        normed[...] = (value * scale * row_of(gain)).astype(BF16)
        got = jnp.dot(normed[...], weight[...], preferred_element_type=F32)
        c, sn = cosine[rows, :], sine[rows, :]
        q, k = got[:, :D] + row_of(q_bias), got[:, D : 2 * D] + key_bias
        kv[s, rows, 0:D] = (k * c + pltpu.roll(k, D // 2, 1) * sn).astype(BF16)
        kv[s, rows, D : 2 * D] = (got[:, 2 * D :] + value_bias).astype(BF16)
        for sg, _ in SIGNS:
            along.send((n, "z", sg), kv_at(n, 0, 0, None), kv_at(n, 0, 0, None), at(sg, 0))
        along.send((n, "c", 0), kv_at(n, 0, 0, None), kv_at(n, 0, 0, None), at(0, 1))
        query[rows, :] = (q * c + pltpu.roll(q, D // 2, 1) * sn).astype(BF16)

    def relay(n):
        for sg, part in SIGNS:
            along.arrived((n, "z", sg), kv_at(n, -sg, 0, None), at(-sg, 0))
            along.send((n, "r", sg), kv_at(n, -sg, 0, part), kv_at(n, -sg, 0, part), at(sg, 0))
            along.send((n, "c", -sg), kv_at(n, -sg, 0, None), kv_at(n, -sg, 0, None), at(0, 1))

    def first():
        for copy in load_qkv:
            copy.wait()
        project(0)

    def third():
        project(2)
        relay(0)

    def fourth():
        relay(1)
        project(3)
        relay(2)

    rows_ref[pl.ds(al(y * RB, RB), RB), own] = shard[...]
    all_gather_2d(
        link, region, "x", lambda half: shard.at[pl.ds(half * HROW, HROW)],
        (first, functools.partial(project, 1), third, fourth),
    )

    step = HEAD_DIMENSION ** (-0.5)
    chunk = 256

    def attend(b, causal):
        keys, values = kv[b, :, 0:D], kv[b, :, D : 2 * D]
        for r in range(TOK_SEQ // chunk):
            rows = slice(r * chunk, (r + 1) * chunk)
            width = (r + 1) * chunk if causal else TOK_SEQ
            score = lax.dot_general(query[rows, :], keys[:width], (((1,), (1,)), ((), ())), preferred_element_type=F32)
            if causal:
                down_row = lax.broadcasted_iota(jnp.int32, score.shape, 0) + r * chunk
                col = lax.broadcasted_iota(jnp.int32, score.shape, 1)
                score = jnp.where(col <= down_row, score, -1e30)
                top = jnp.max(score, axis=1, keepdims=True)
                p = jnp.exp((score - top) * step)
                total[rows, :] = jnp.sum(p, axis=1, keepdims=True)
                acc[rows, :] = jnp.dot(p.astype(BF16), values[:width], preferred_element_type=F32)
            else:
                old = best[rows, :]
                top = jnp.maximum(old, jnp.max(score, axis=1, keepdims=True))
                fade = jnp.exp((old - top) * step)
                p = jnp.exp((score - top) * step)
                total[rows, :] = total[rows, :] * fade + jnp.sum(p, axis=1, keepdims=True)
                acc[rows, :] = acc[rows, :] * fade + jnp.dot(p.astype(BF16), values, preferred_element_type=F32)
            best[rows, :] = top

    def attend_if(dz, dc):
        b = at(dz, dc)

        @pl.when(b < s)
        def _():
            attend(b, False)

    attend(s, True)
    relay(3)
    for n in range(4):
        along.arrived((n, "c", 0), kv_at(n, 0, 1, None), at(0, 1))
    attend_if(0, 1)
    for n in range(4):
        for sg, part in SIGNS:
            along.arrived((n, "r", sg), kv_at(n, 2, 0, part), at(-sg, 0))
            along.send((n, "c", 2, part), kv_at(n, 2, 0, part), kv_at(n, 2, 0, part), at(0, 1))
    for dz in (-1, 1):
        attend_if(dz, 0)
        for n in range(4):
            along.arrived((n, "c", dz), kv_at(n, dz, 1, None), at(0, 1))
        attend_if(dz, 1)
    attend_if(2, 0)
    for n in range(4):
        for part in (0, 1):
            along.arrived((n, "c", 2, part), kv_at(n, 2, 1, part), at(0, 1))
    attend_if(2, 1)
    heads[:, pl.ds(al(t * D, 128), D)] = (acc[...] / total[...]).astype(BF16)

    def head_region(half, x, y, part):
        first, count = ((0, 256), (0, 128), (128, 128))[0 if part is None else 1 + part]
        return heads.at[pl.ds(half * 256 + first, count), pl.ds(al((x * SIDE + y) * D, 128), D)]

    all_gather_2d(link, head_region, "h")
    for dz in (0, -1, 1):
        along.arrived(("o", "c", dz), o_region(dz, 1, None), at(0, 1))
    for part in (0, 1):
        along.arrived(("o", "c", 2, part), o_region(2, 1, part), at(0, 1))
    mine = lax.dot_general(rows_ref[:, own], spot, (((1,), (1,)), ((), ())), preferred_element_type=F32)
    last = o_cols[...].reshape(LOCAL_QUERY_HEAD * D, COLS)
    out[...] = (mine + jnp.dot(heads[...], last, preferred_element_type=F32)).astype(BF16)
    link.drain()
    along.drain()


LINKS = 3 * AG_SEMS + 30 + 24
ALONG = 45


def run(*operands):
    vmem = pl.BlockSpec(memory_space=pltpu.VMEM)
    hbm = pl.BlockSpec(memory_space=pl.ANY)
    smem = pl.BlockSpec(memory_space=pltpu.SMEM)

    def b16(*shape):
        return pltpu.VMEM(shape, BF16)

    def f32(*shape):
        return pltpu.VMEM(shape, F32)

    return pl.pallas_call(
        body,
        out_shape=jax.ShapeDtypeStruct((TOK_SEQ, COLS), BF16),
        in_specs=[
            smem, vmem, vmem, vmem, hbm, vmem, hbm, vmem, vmem, vmem, hbm, vmem, hbm, vmem, hbm, vmem, vmem
        ],
        out_specs=vmem,
        scratch_shapes=[
            b16(HID, MW), b16(HID, WIDTH), b16(16, WIDTH), b16(N_TP, 16, COLS), b16(N_TP, D, COLS),
            b16(N_TP, 32, TCOL), b16(N_TP, 32, TCOL), b16(ROWS, MW), f32(ROWS, HID), b16(TOK_SEQ, HID),
            b16(SIDE, HROW, WIDTH), b16(SIDE, HROW, WIDTH),
            b16(2, 2, HROW, BLK), b16(2, SIDE, HROW, BLK), b16(2, 2, HROW, BLK), b16(SIDE, HROW, BLK),
            b16(2, HROW, WIDTH // 2), b16(2, HROW, WIDTH), b16(2, HROW, WIDTH // 2), b16(HROW, WIDTH),
            b16(2, 2, QROW, BLK), b16(2, 2, 2, QROW, BLK), b16(2, 2, QROW, BLK), b16(RB, BLK),
            b16(TOK_SEQ, WIDTH), b16(WIDTH, 3 * D), b16(RB, WIDTH), b16(TOK_SEQ, D), b16(N_SEQ, TOK_SEQ, 2 * D),
            b16(TOK_SEQ, LOCAL_QUERY_HEAD * D), f32(TOK_SEQ, 1), f32(TOK_SEQ, 1), f32(TOK_SEQ, D),
            pltpu.SemaphoreType.DMA((6,)),
            pltpu.SemaphoreType.DMA((LINKS,)), pltpu.SemaphoreType.DMA((LINKS,)),
            pltpu.SemaphoreType.DMA((ALONG,)), pltpu.SemaphoreType.DMA((ALONG,)),
        ],
        compiler_params=pltpu.CompilerParams(
            collective_id=0, has_side_effects=True, vmem_limit_bytes=60 * 1024 * 1024
        ),
        name="block",
    )(*operands)


def image_fields(image_table):
    grid_h = image_table[:, 0]
    grid_w = image_table[:, 1]
    across = grid_w // 2
    return (across, grid_h // 2 * across, image_table[:, 2])


def rope_tables(positions, across, counts, offsets, head_size):
    inside = (
        (positions[:, None] >= offsets[None, :]) & (positions[:, None] < (offsets + counts)[None, :])
    ).astype(jnp.int32)
    is_image = jnp.sum(inside, axis=1)
    run_start = jnp.sum(inside * offsets[None, :], axis=1)
    row_width = jnp.sum(inside * across[None, :], axis=1) + (1 - is_image)
    inner_index = positions - run_start
    pos_t = jnp.where(is_image > 0, run_start, positions)
    pos_h = jnp.where(is_image > 0, run_start + inner_index // row_width, positions)
    pos_w = jnp.where(is_image > 0, run_start + inner_index % row_width, positions)
    half_size = head_size // 2
    frequency = jnp.arange(half_size, dtype=jnp.int32)
    inverse = THETA ** (-2.0 * frequency.astype(F32) / head_size)
    first_cut = head_size // 8
    second_cut = first_cut + 3 * head_size // 16
    chosen = jnp.where(
        frequency[None, :] < first_cut,
        pos_t[:, None],
        jnp.where(frequency[None, :] < second_cut, pos_h[:, None], pos_w[:, None]),
    )
    angles = chosen.astype(F32) * inverse[None, :]
    cosine, sine = jnp.cos(angles), jnp.sin(angles)
    return (jnp.concatenate([cosine, cosine], axis=1), jnp.concatenate([-sine, sine], axis=1))


def per_device(
    patches, image_table, ln_gain, ln_bias, merge_up, merge_up_bias, merge_down, merge_down_bias,
    text_embeds, attn_gain, q_weight, q_bias, key_value_weight, key_value_bias, o_weight,
):
    seq_index = lax.axis_index("seq")
    positions = seq_index * TOK_SEQ + jnp.arange(TOK_SEQ, dtype=jnp.int32)
    begin = 2 * seq_index * N_TP
    group = lax.dynamic_slice_in_dim(image_table, begin, 2 * N_TP)
    across, counts, offsets = image_fields(group)
    cosine, sine = rope_tables(positions, across, counts, offsets, HEAD_DIMENSION)
    return run(
        image_table.T, patches, ln_gain, ln_bias, merge_up.T, merge_up_bias, merge_down, merge_down_bias,
        text_embeds.T, attn_gain, q_weight, q_bias, key_value_weight, key_value_bias, o_weight, cosine, sine,
    )


def solution(mesh):
    return jax.shard_map(
        per_device,
        mesh=mesh,
        in_specs=(
            P(("seq", "tp"), None),
            P(),
            P(),
            P(),
            P(None, "tp"),
            P("tp"),
            P("tp", None),
            P(),
            P("seq", "tp"),
            P(),
            P(None, "tp"),
            P("tp"),
            P(),
            P(),
            P("tp", None),
        ),
        out_specs=P("seq", "tp"),
        check_vma=False,
    )
```

time: 213 us -> 136 us (0.64); the launches traced: 211 us -> 136 us
  matrix products: 19.3 us -> 0 us
  other arithmetic: 20.1 us -> 3 us
  Pallas kernels: 147 us -> 130 us
  local copies, waits for them, and re-layouts: 16.3 us -> 2.54 us
  starting transfers between devices: 7.03 us -> 0 us
    dot_general x6 -> x0, matrix products: 19.3 us -> none  [the longest x1 3.96 us: per_device(): jnp.einsum('qd,kd->qk', query, keys, preferred_element_type=F32)]
    pallas_call x4 -> x1, Pallas kernels: 147 us -> 130 us  [run(): pl.pallas_call(body, out_shape=jax.ShapeDtypeStruct((TOK_SEQ, COLS), BF16...]
    unnamed x15 -> x0, local copies, waits for them, and re-layouts: 9.32 us -> none
    convert_element_type x2 -> x0, other arithmetic: 7.25 us -> none  [the longest x1 5.83 us: per_device(): (residual * scale_rows[:, None] * attn_gain[None, :]).astype(BF16)]
    all_to_all x1 -> x0, starting transfers between devices: 7.03 us -> none  [per_device(): lax.all_to_all(o_weight, 'tp', split_axis=1, concat_axis=0, tiled=True)]
    reduce_sum x6 -> x1, other arithmetic: 6.67 us -> 0.11 us  [rope_tables(): is_image = jnp.sum(inside, axis=1)]
    select_n x7 -> x0, other arithmetic: 4.57 us -> none  [the longest x1 0.98 us: per_device(): jnp.where(is_image > 0, compact % 2 * 2 * HALF + compact // 2, -1)]
    reshape x3 -> x0, local copies, waits for them, and re-layouts: 3.11 us -> none  [the longest x1 1.29 us: per_device(): ln_bias.reshape(1, VW)]
  transfers between devices with their start and end apart: 1 -> 0, of which waited for: 0 -> 0; matrix products, arithmetic and copies ran while one was open for 24% -> 0% of each run, Pallas kernels for 70% -> 0%
where the time goes in v2:
time: 136 us
  Pallas kernels  130 us (96%)
  other arithmetic  3 us (2%)
  local copies, waits for them, and re-layouts  2.54 us (2%)
    pallas_call x1, Pallas kernels, run(): pl.pallas_call(body, out_shape=jax.ShapeDtypeStruct((TOK_SEQ, COLS), BF16...  130 us

profile of v2, /device:TPU:96, one launch (start us, length us, event | category | flops | bytes accessed | tf_op | source)
XLA Modules:
  0.0 135.8 jit_solution(6356602773051014152)
XLA Ops:
  0.0 0.8 constant_dynamic-slice_fusion
  0.8 0.1 convert_reduce_fusion
  0.9 0.1 fusion.4
  1.1 1.7 %fusion.2 = (f32[512,64]{1,0:T(8,128)S(1)}, f32[512,64]{1,0:T(8,128)S(1)}, f32[512,64]{1,0:T(8,128)S(1)}) fusion(f32[64]{0:T(128)S(1)} %multiply_power_fusion, s32[512]{0:T(512)S(1)} %get-tuple-element.14, s32[512]{0:T(512)S(1)} %get-tuple-element.13, pred[64]{0:T(512)(128)(4,1)S(1)} %iota_compare_fusion, s32[512]{0:T(512)S(1)} %get-tuple-element.15, ...), kind=kLoop, calls=%fused_computation.9 | loop fusion | flops 163840 | bytes 399744 | tf_op jit(solution)/shard_map/neg | solution.py:665
  2.8 1.0 pad_maximum_fusion
  3.8 130.3 %block.1 = bf16[512,224]{1,0:T(8,128)(2,1)} custom-call(s32[3,256]{1,0:T(4,128)} %bitcast.28, bf16[256,1280]{1,0:T(8,128)(2,1)} %patches.1, f32[1280]{0:T(1024)} %ln_gain.1, f32[1280]{0:T(1024)} %ln_bias.1, bf16[320,5120]{1,0:T(8,128)(2,1)} %bitcast.26, f32[320]{0:T(512)} %up_bias.1, bf16[320,3584]{1,0:T(8,128)(2,1)} %down_hbm.1, f32[3584]{0:T(1024)} %down_bias.1, ...), custom_call_target="tpu_custom_call" | custom-call | tf_op jit(solution)/shard_map/block/pallas_call | solution.py:608
  134.1 1.8 %copy.17 = bf16[512,224]{0,1:T(8,128)(2,1)} copy(bf16[512,224]{1,0:T(8,128)(2,1)} %block.1) | data formatting | bytes 458752 | tf_op jit(solution)/shard_map/block/pallas_call | solution.py:608
  (6 shorter events, 0.0 us)

commit v3 on v2

--- a/solution.py
+++ b/solution.py
@@ -2,6 +2,7 @@
 
 import jax
 import jax.numpy as jnp
+import numpy as np
 from jax import lax
 from jax.experimental import pallas as pl
 from jax.experimental.pallas import tpu as pltpu
@@ -194,11 +195,11 @@
 
 
 def body(
-    table, patches, ln_gain, ln_bias, up_hbm, up_bias, down_hbm, down_bias, text, gain, q_weight, q_bias,
-    kv_weight, kv_bias, o_hbm, cosine, sine, out,
+    table, patches_hbm, ln_gain, ln_bias, up_hbm, up_bias, down_hbm, down_bias, text_hbm, gain, q_weight, q_bias,
+    kv_weight, kv_bias, o_hbm, frequency, out,
     up, down, o_rows, o_send, o_cols, outgoing, incoming, tokens, lifted, hidden, pa, pb,
     a_raw, a_mid, a_out, a_sum, b_raw, b_mid, b_out, b_sum, c_raw, c_mid, c_out, shard,
-    rows_ref, weight, normed, query, kv, heads, best, total, acc, load_sem, send_sem, recv_sem, seq_send, seq_recv,
+    rows_ref, weight, normed, query, kv, heads, best, total, acc, pick_ref, cosine, sine, out_turned, out_sum, patches, text, load_sem, send_sem, recv_sem, seq_send, seq_recv,
 ):
     t, x, y = place()
     s = lax.axis_index("seq")
@@ -218,18 +219,13 @@
         copy.start()
         return copy
 
+    load_patches = load(6, patches_hbm, patches)
     load_o = load(0, o_hbm.at[pl.ds(al(s * 16, 16), 16), :], o_rows)
-    load_up = load(1, up_hbm, up)
-    load_down = load(2, down_hbm, down)
-    load_qkv = [
-        load(3, q_weight, weight.at[:, pl.ds(0, D)]),
-        load(4, kv_weight.at[:, pl.ds(al(x * D, 128), D)], weight.at[:, pl.ds(D, D)]),
-        load(5, kv_weight.at[:, pl.ds(al((KEY_VALUE_HEADS + x) * D, 128), D)], weight.at[:, pl.ds(2 * D, D)]),
-    ]
     link = Link(send_sem, recv_sem)
     along = Link(seq_send, seq_recv, "seq")
     start, length, base = layout(table, s)
 
+    load_patches.wait()
     value = patches[...].astype(F32)
     centre = jnp.mean(value, axis=-1, keepdims=True)
     centred = value - centre
@@ -263,6 +259,15 @@
         link.send(("o", o), o_send.at[to], o_cols.at[t, o_place, :], to)
     o_cols[t, o_place, :] = o_send[t]
 
+    load_up = load(1, up_hbm, up)
+    load_down = load(2, down_hbm, down)
+    load_text = load(7, text_hbm, text)
+    load_qkv = [
+        load(3, q_weight, weight.at[:, pl.ds(0, D)]),
+        load(4, kv_weight.at[:, pl.ds(al(x * D, 128), D)], weight.at[:, pl.ds(D, D)]),
+        load(5, kv_weight.at[:, pl.ds(al((KEY_VALUE_HEADS + x) * D, 128), D)], weight.at[:, pl.ds(2 * D, D)]),
+    ]
+
     half_of = lax.rem(t, 2)
     lane = lax.broadcasted_iota(jnp.int32, (1, N_TP * 32), 1)
     base_row = jnp.zeros((1, N_TP * 32), jnp.int32)
@@ -295,6 +300,58 @@
         first, count = ((0, N_TP), (0, 8), (8, 8))[0 if part is None else 1 + part]
         return o_cols.at[pl.ds(first, count), pl.ds(al(at(dz, dc) * 16, 16), 16), :]
 
+    spot = (
+        lax.broadcasted_iota(jnp.int32, (COLS, BLK), 0) + y * COLS == lax.broadcasted_iota(jnp.int32, (COLS, BLK), 1)
+    ).astype(BF16)
+    own = pl.ds(al(x * BLK, 128), BLK)
+    at_lane = s * TOK_SEQ + lax.broadcasted_iota(jnp.int32, (1, TOK_SEQ), 1)
+
+    def find_rows():
+        order = lax.broadcasted_iota(jnp.int32, (TOK_SEQ, 1), 0)
+        pos = s * TOK_SEQ + lax.rem(order, 256) // HROW * RB + order // 256 * HROW + lax.rem(order, HROW)
+        where = jnp.full((TOK_SEQ, 1), -1, jnp.int32)
+        for e in range(N_TP):
+            inner = pos - start[e]
+            where = jnp.where((inner >= 0) & (inner < length[e]), base[e] + inner, where)
+        where = jnp.where(where >= 0, lax.rem(where, 2) * 2 * HALF + where // 2, -1)
+        pick_ref[...] = (lax.broadcasted_iota(jnp.int32, (TOK_SEQ, ROWS), 1) == where).astype(BF16)
+
+    def find_words():
+        load_text.wait()
+        plain = jnp.ones((1, TOK_SEQ), F32)
+        for e in range(N_TP):
+            plain = jnp.where((at_lane >= start[e]) & (at_lane < start[e] + length[e]), 0.0, plain)
+        words = (text[...].astype(F32) * plain).astype(BF16)
+        for rb in range(SIDE):
+            add = lax.dot_general(
+                words[:, rb * RB : (rb + 1) * RB], spot, (((0,), (0,)), ((), ())), preferred_element_type=F32
+            ).astype(BF16)
+            a_sum[rb] = add[:HROW]
+            b_sum[:, rb * BLK : (rb + 1) * BLK] = add[HROW:]
+
+    def find_angles():
+        run, across = at_lane, jnp.ones((1, TOK_SEQ), jnp.int32)
+        for i in range(2 * N_TP):
+            k = 2 * N_TP * s + i
+            first, width = table[2, k], table[1, k] // 2
+            inside = (at_lane >= first) & (at_lane < first + (table[0, k] // 2) * width)
+            run = jnp.where(inside, first, run)
+            across = jnp.where(inside, width, across)
+        inner = (at_lane - run).astype(F32)
+        wide = across.astype(F32)
+        line = jnp.floor((inner + 0.5) / wide)
+        begin = run.astype(F32)
+        stack = jnp.concatenate(
+            [begin, begin + line, begin + (inner - line * wide), jnp.zeros((5, TOK_SEQ), F32)], axis=0
+        )
+        turned = jnp.transpose(stack)
+        f = lax.rem(lax.broadcasted_iota(jnp.int32, (1, D), 1), D // 2)
+        position = jnp.where(f < 16, turned[:, 0:1], jnp.where(f < 40, turned[:, 1:2], turned[:, 2:3]))
+        angle = position * frequency[...]
+        cosine[...] = jnp.cos(angle)
+        lane = lax.broadcasted_iota(jnp.int32, (1, D), 1)
+        sine[...] = jnp.sin(angle) * jnp.where(lane < D // 2, -1.0, 1.0)
+
     def lift(n):
         cols = pl.ds(al(wrap(x + ORDER[n]) * VW, 128), VW)
         got = lax.dot_general(
@@ -314,57 +371,29 @@
         for sg, _ in SIGNS:
             along.send(("o", "z", sg), o_region(0, 0, None), o_region(0, 0, None), at(sg, 0))
         along.send(("o", "c", 0), o_region(0, 0, None), o_region(0, 0, None), at(0, 1))
+        find_rows()
+
+    def lift_second():
+        lift(1)
+        find_angles()
+
+    def lift_third():
+        lift(2)
+        find_words()
 
     all_gather_2d(
-        link, token_region, "t", None,
-        (lift_first, functools.partial(lift, 1), functools.partial(lift, 2), functools.partial(lift, 3)), 1,
+        link, token_region, "t", None, (lift_first, lift_second, lift_third, functools.partial(lift, 3)), 1
     )
 
     raised = lifted[...]
     act = (0.5 * raised * (1.0 + lax.erf(raised * 0.5**0.5))).astype(BF16)
-    order = lax.broadcasted_iota(jnp.int32, (TOK_SEQ, 1), 0)
-    pos = s * TOK_SEQ + lax.rem(order, 256) // HROW * RB + order // 256 * HROW + lax.rem(order, HROW)
-    where = jnp.full((TOK_SEQ, 1), -1, jnp.int32)
-    for e in range(N_TP):
-        inner = pos - start[e]
-        where = jnp.where((inner >= 0) & (inner < length[e]), base[e] + inner, where)
-    where = jnp.where(where >= 0, lax.rem(where, 2) * 2 * HALF + where // 2, -1)
-    pick = (lax.broadcasted_iota(jnp.int32, (TOK_SEQ, ROWS), 1) == where).astype(BF16)
-    hidden[...] = jnp.dot(pick, act, preferred_element_type=F32).astype(BF16)
+    hidden[...] = jnp.dot(pick_ref[...], act, preferred_element_type=F32).astype(BF16)
     load_down.wait()
-    spot = (
-        lax.broadcasted_iota(jnp.int32, (COLS, BLK), 0) + y * COLS == lax.broadcasted_iota(jnp.int32, (COLS, BLK), 1)
-    ).astype(BF16)
-    own = pl.ds(al(x * BLK, 128), BLK)
-    at_lane = s * TOK_SEQ + lax.broadcasted_iota(jnp.int32, (1, TOK_SEQ), 1)
-    plain = jnp.ones((1, TOK_SEQ), F32)
-    for e in range(N_TP):
-        plain = jnp.where((at_lane >= start[e]) & (at_lane < start[e] + length[e]), 0.0, plain)
-    words = (text[...].astype(F32) * plain).astype(BF16)
-
-    def words_of(rb):
-        return lax.dot_general(
-            words[:, rb * RB : (rb + 1) * RB], spot, (((0,), (0,)), ((), ())), preferred_element_type=F32
-        )
-
     def lower_a(i):
         cols = pl.ds(al(wrap(x + i) * BLK, 128), BLK)
         got = jnp.dot(hidden[0:256, :], down[:, cols], preferred_element_type=F32)
         pa[:, :, cols] = got.astype(BF16).reshape(SIDE, HROW, BLK)
 
-    def lower_b(i):
-        rb = wrap(y + i)
-        got = jnp.dot(hidden[pl.ds(al(256 + rb * HROW, HROW), HROW), :], down[...], preferred_element_type=F32)
-        pb[rb] = got.astype(BF16)
-
-    for rb in range(SIDE):
-        add = words_of(rb)
-        a_add = add[:HROW]
-        pb_add = add[HROW:]
-        a_sum[rb] = a_add.astype(BF16)
-        b_words = pb_add.astype(BF16)
-        b_sum[pl.ds(0, HROW), pl.ds(rb * BLK, BLK)] = b_words
-
     def a_piece(i, part):
         rows = (pl.ds(0, SIDE), pl.ds(0, 2), pl.ds(2, 2))[0 if part is None else 1 + part]
         return pa.at[rows, :, pl.ds(al(wrap(x + i) * BLK, 128), BLK)]
@@ -389,31 +418,39 @@
         if i == 0:
             pa[:, :, own] = (pa[:, :, own].astype(F32) + a_sum[...].astype(F32)).astype(BF16)
 
-    def make_b(i):
-        lower_b(i)
-        rb = wrap(y + i)
-        add = b_sum[:, pl.ds(al(rb * BLK, 128), BLK)].astype(F32)
-        pb[rb, :, own] = (pb[rb, :, own].astype(F32) + add).astype(BF16)
-
-    sides = (
-        ("a", a_piece, a_raw, a_mid, a_out, to_x, make_a),
-        ("b", b_piece, b_raw, b_mid, b_out, to_y, make_b),
-    )
-    for n, piece, raw, mid, outb, to, make in sides:
-        make(2)
+    def make_b():
+        for c in range(SIDE):
+            cols = slice(c * BLK, (c + 1) * BLK)
+            got = jnp.dot(hidden[256:, :], down[:, cols], preferred_element_type=F32)
+            pb[:, :, cols] = got.astype(BF16).reshape(SIDE, HROW, BLK)
+        for rb in range(SIDE):
+            add = b_sum[:, rb * BLK : (rb + 1) * BLK].astype(F32)
+            pb[rb, :, own] = (pb[rb, :, own].astype(F32) + add).astype(BF16)
+
+    sides = (("a", a_piece, a_raw, a_mid, a_out, to_x), ("b", b_piece, b_raw, b_mid, b_out, to_y))
+
+    def send_raw(n, piece, raw, mid, outb, to):
         for sg, part in SIGNS:
             link.send((n, "raw", sg), piece(2, part), raw.at[part], to(sg))
+
+    def send_own(sg, part, n, piece, raw, mid, outb, to):
+        link.send((n, "own", sg), piece(sg, 1 - part), mid_of(mid.at[part], n, 1 - part), to(sg))
+
+    make_a(2)
+    send_raw(*sides[0])
+    make_b()
+    send_raw(*sides[1])
     for sg, part in SIGNS:
-        for n, piece, raw, mid, outb, to, make in sides:
-            make(sg)
-            link.send((n, "own", sg), piece(sg, 1 - part), mid_of(mid.at[part], n, 1 - part), to(sg))
-    for n, piece, raw, mid, outb, to, make in sides:
+        send_own(sg, part, *sides[1])
+    for sg, part in SIGNS:
+        make_a(sg)
+        send_own(sg, part, *sides[0])
+    for n, piece, raw, mid, outb, to in sides:
         for sg, part in SIGNS:
             link.arrived((n, "raw", sg), raw.at[part], to(-sg))
             outb[part] = (raw[part].astype(F32) + piece(sg, part)[...].astype(F32)).astype(BF16)
             link.send((n, "sum", sg), outb.at[part], mid_of(mid.at[part], n, part), to(sg))
-    for n, piece, raw, mid, outb, to, make in sides:
-        make(0)
+    make_a(0)
 
     for sg, part in SIGNS:
         along.arrived(("o", "z", sg), o_region(-sg, 0, None), at(-sg, 0))
@@ -430,7 +467,7 @@
 
     after = ((0, a_next, to_y), (1, b_next, to_x))
     for side, nxt in zip(sides, after):
-        n, piece, raw, mid, outb, to, make = side
+        n, piece, raw, mid, outb, to = side
         for sg, part in SIGNS:
             link.arrived((n, "own", sg), mid_of(mid.at[part], n, 1 - part), to(-sg))
             link.arrived((n, "sum", sg), mid_of(mid.at[part], n, part), to(-sg))
@@ -471,9 +508,8 @@
             pl.ds(al(x * BLK, 128), BLK),
         ]
 
-    def kv_at(n, dz, dc, part):
-        first, count = ((0, RB), (0, HROW), (HROW, HROW))[0 if part is None else 1 + part]
-        return kv.at[at(dz, dc), pl.ds(al(wrap(y + ORDER[n]) * RB + first, HROW), count), :]
+    def kv_at(n, dz, dc):
+        return kv.at[at(dz, dc), pl.ds(al(wrap(y + ORDER[n]) * RB, RB), RB), :]
 
     kv_row = row_of(kv_bias)
     heads_of = [kv_row[:, k * D : (k + 1) * D] for k in range(2 * KEY_VALUE_HEADS)]
@@ -490,15 +526,15 @@
         kv[s, rows, 0:D] = (k * c + pltpu.roll(k, D // 2, 1) * sn).astype(BF16)
         kv[s, rows, D : 2 * D] = (got[:, 2 * D :] + value_bias).astype(BF16)
         for sg, _ in SIGNS:
-            along.send((n, "z", sg), kv_at(n, 0, 0, None), kv_at(n, 0, 0, None), at(sg, 0))
-        along.send((n, "c", 0), kv_at(n, 0, 0, None), kv_at(n, 0, 0, None), at(0, 1))
+            along.send((n, "z", sg), kv_at(n, 0, 0), kv_at(n, 0, 0), at(sg, 0))
+        along.send((n, "z", 2), kv_at(n, 0, 0), kv_at(n, 0, 0), at(2, 0))
+        along.send((n, "c", 0), kv_at(n, 0, 0), kv_at(n, 0, 0), at(0, 1))
         query[rows, :] = (q * c + pltpu.roll(q, D // 2, 1) * sn).astype(BF16)
 
-    def relay(n):
-        for sg, part in SIGNS:
-            along.arrived((n, "z", sg), kv_at(n, -sg, 0, None), at(-sg, 0))
-            along.send((n, "r", sg), kv_at(n, -sg, 0, part), kv_at(n, -sg, 0, part), at(sg, 0))
-            along.send((n, "c", -sg), kv_at(n, -sg, 0, None), kv_at(n, -sg, 0, None), at(0, 1))
+    def relay(n, steps):
+        for dz in steps:
+            along.arrived((n, "z", -dz if dz != 2 else 2), kv_at(n, dz, 0), at(dz, 0))
+            along.send((n, "c", dz), kv_at(n, dz, 0), kv_at(n, dz, 0), at(0, 1))
 
     def first():
         for copy in load_qkv:
@@ -507,12 +543,12 @@
 
     def third():
         project(2)
-        relay(0)
+        relay(0, (-1, 1, 2))
 
     def fourth():
-        relay(1)
+        relay(1, (-1, 1, 2))
         project(3)
-        relay(2)
+        relay(2, (-1, 1, 2))
 
     rows_ref[pl.ds(al(y * RB, RB), RB), own] = shard[...]
     all_gather_2d(
@@ -554,44 +590,48 @@
             attend(b, False)
 
     attend(s, True)
-    relay(3)
+    relay(3, (-1, 1))
     for n in range(4):
-        along.arrived((n, "c", 0), kv_at(n, 0, 1, None), at(0, 1))
+        along.arrived((n, "c", 0), kv_at(n, 0, 1), at(0, 1))
     attend_if(0, 1)
-    for n in range(4):
-        for sg, part in SIGNS:
-            along.arrived((n, "r", sg), kv_at(n, 2, 0, part), at(-sg, 0))
-            along.send((n, "c", 2, part), kv_at(n, 2, 0, part), kv_at(n, 2, 0, part), at(0, 1))
-    for dz in (-1, 1):
+    relay(3, (2,))
+    for dz in (-1, 1, 2):
         attend_if(dz, 0)
         for n in range(4):
-            along.arrived((n, "c", dz), kv_at(n, dz, 1, None), at(0, 1))
+            along.arrived((n, "c", dz), kv_at(n, dz, 1), at(0, 1))
         attend_if(dz, 1)
-    attend_if(2, 0)
-    for n in range(4):
-        for part in (0, 1):
-            along.arrived((n, "c", 2, part), kv_at(n, 2, 1, part), at(0, 1))
-    attend_if(2, 1)
     heads[:, pl.ds(al(t * D, 128), D)] = (acc[...] / total[...]).astype(BF16)
 
     def head_region(half, x, y, part):
         first, count = ((0, 256), (0, 128), (128, 128))[0 if part is None else 1 + part]
         return heads.at[pl.ds(half * 256 + first, count), pl.ds(al((x * SIDE + y) * D, 128), D)]
 
-    all_gather_2d(link, head_region, "h")
-    for dz in (0, -1, 1):
-        along.arrived(("o", "c", dz), o_region(dz, 1, None), at(0, 1))
-    for part in (0, 1):
-        along.arrived(("o", "c", 2, part), o_region(2, 1, part), at(0, 1))
-    mine = lax.dot_general(rows_ref[:, own], spot, (((1,), (1,)), ((), ())), preferred_element_type=F32)
-    last = o_cols[...].reshape(LOCAL_QUERY_HEAD * D, COLS)
-    out[...] = (mine + jnp.dot(heads[...], last, preferred_element_type=F32)).astype(BF16)
+    def mix(n):
+        if n == 0:
+            for dz in (0, -1, 1):
+                along.arrived(("o", "c", dz), o_region(dz, 1, None), at(0, 1))
+            for part in (0, 1):
+                along.arrived(("o", "c", 2, part), o_region(2, 1, part), at(0, 1))
+            out_turned[...] = jnp.transpose(o_cols[...].reshape(LOCAL_QUERY_HEAD * D, COLS))
+            out_sum[...] = lax.dot_general(
+                spot, rows_ref[:, own], (((1,), (1,)), ((), ())), preferred_element_type=F32
+            )
+        cols = pl.ds(al(wrap(x + ORDER[n]) * SIDE * D, 128), SIDE * D)
+        got = lax.dot_general(
+            out_turned[:, cols], heads[:, cols], (((1,), (1,)), ((), ())), preferred_element_type=F32
+        )
+        if n < 3:
+            out_sum[...] += got
+        else:
+            out[...] = (out_sum[...] + got).astype(BF16)
+
+    all_gather_2d(link, head_region, "h", None, [functools.partial(mix, n) for n in range(4)], 1)
     link.drain()
     along.drain()
 
 
 LINKS = 3 * AG_SEMS + 30 + 24
-ALONG = 45
+ALONG = 9 + 28
 
 
 def run(*operands):
@@ -607,9 +647,9 @@
 
     return pl.pallas_call(
         body,
-        out_shape=jax.ShapeDtypeStruct((TOK_SEQ, COLS), BF16),
+        out_shape=jax.ShapeDtypeStruct((COLS, TOK_SEQ), BF16),
         in_specs=[
-            smem, vmem, vmem, vmem, hbm, vmem, hbm, vmem, vmem, vmem, hbm, vmem, hbm, vmem, hbm, vmem, vmem
+            smem, hbm, vmem, vmem, hbm, vmem, hbm, vmem, hbm, vmem, hbm, vmem, hbm, vmem, hbm, vmem
         ],
         out_specs=vmem,
         scratch_shapes=[
@@ -621,7 +661,9 @@
             b16(2, 2, QROW, BLK), b16(2, 2, 2, QROW, BLK), b16(2, 2, QROW, BLK), b16(RB, BLK),
             b16(TOK_SEQ, WIDTH), b16(WIDTH, 3 * D), b16(RB, WIDTH), b16(TOK_SEQ, D), b16(N_SEQ, TOK_SEQ, 2 * D),
             b16(TOK_SEQ, LOCAL_QUERY_HEAD * D), f32(TOK_SEQ, 1), f32(TOK_SEQ, 1), f32(TOK_SEQ, D),
-            pltpu.SemaphoreType.DMA((6,)),
+            b16(TOK_SEQ, ROWS), f32(TOK_SEQ, D), f32(TOK_SEQ, D), b16(COLS, LOCAL_QUERY_HEAD * D), f32(COLS, TOK_SEQ),
+            b16(4 * CAP, VW), b16(COLS, TOK_SEQ),
+            pltpu.SemaphoreType.DMA((8,)),
             pltpu.SemaphoreType.DMA((LINKS,)), pltpu.SemaphoreType.DMA((LINKS,)),
             pltpu.SemaphoreType.DMA((ALONG,)), pltpu.SemaphoreType.DMA((ALONG,)),
         ],
@@ -632,53 +674,17 @@
     )(*operands)
 
 
-def image_fields(image_table):
-    grid_h = image_table[:, 0]
-    grid_w = image_table[:, 1]
-    across = grid_w // 2
-    return (across, grid_h // 2 * across, image_table[:, 2])
-
-
-def rope_tables(positions, across, counts, offsets, head_size):
-    inside = (
-        (positions[:, None] >= offsets[None, :]) & (positions[:, None] < (offsets + counts)[None, :])
-    ).astype(jnp.int32)
-    is_image = jnp.sum(inside, axis=1)
-    run_start = jnp.sum(inside * offsets[None, :], axis=1)
-    row_width = jnp.sum(inside * across[None, :], axis=1) + (1 - is_image)
-    inner_index = positions - run_start
-    pos_t = jnp.where(is_image > 0, run_start, positions)
-    pos_h = jnp.where(is_image > 0, run_start + inner_index // row_width, positions)
-    pos_w = jnp.where(is_image > 0, run_start + inner_index % row_width, positions)
-    half_size = head_size // 2
-    frequency = jnp.arange(half_size, dtype=jnp.int32)
-    inverse = THETA ** (-2.0 * frequency.astype(F32) / head_size)
-    first_cut = head_size // 8
-    second_cut = first_cut + 3 * head_size // 16
-    chosen = jnp.where(
-        frequency[None, :] < first_cut,
-        pos_t[:, None],
-        jnp.where(frequency[None, :] < second_cut, pos_h[:, None], pos_w[:, None]),
-    )
-    angles = chosen.astype(F32) * inverse[None, :]
-    cosine, sine = jnp.cos(angles), jnp.sin(angles)
-    return (jnp.concatenate([cosine, cosine], axis=1), jnp.concatenate([-sine, sine], axis=1))
-
-
 def per_device(
     patches, image_table, ln_gain, ln_bias, merge_up, merge_up_bias, merge_down, merge_down_bias,
     text_embeds, attn_gain, q_weight, q_bias, key_value_weight, key_value_bias, o_weight,
 ):
-    seq_index = lax.axis_index("seq")
-    positions = seq_index * TOK_SEQ + jnp.arange(TOK_SEQ, dtype=jnp.int32)
-    begin = 2 * seq_index * N_TP
-    group = lax.dynamic_slice_in_dim(image_table, begin, 2 * N_TP)
-    across, counts, offsets = image_fields(group)
-    cosine, sine = rope_tables(positions, across, counts, offsets, HEAD_DIMENSION)
+    half = D // 2
+    powers = np.float32(THETA) ** (np.float32(-2.0) * np.arange(half, dtype=np.float32) / np.float32(D))
+    frequency = jnp.asarray(np.concatenate([powers, powers]).astype(np.float32).reshape(1, D))
     return run(
         image_table.T, patches, ln_gain, ln_bias, merge_up.T, merge_up_bias, merge_down, merge_down_bias,
-        text_embeds.T, attn_gain, q_weight, q_bias, key_value_weight, key_value_bias, o_weight, cosine, sine,
-    )
+        text_embeds.T, attn_gain, q_weight, q_bias, key_value_weight, key_value_bias, o_weight, frequency,
+    ).T
 
 
 def solution(mesh):

time: 136 us -> 130 us (0.956)
  other arithmetic: 3 us -> 0 us
  Pallas kernels: 130 us -> 128 us
    pallas_call x1, Pallas kernels: 130 us -> 128 us  [run(): pl.pallas_call(body, out_shape=jax.ShapeDtypeStruct((COLS, TOK_SEQ), BF16...]
    pallas_call x1 -> x0, local copies, waits for them, and re-layouts: 1.77 us -> none  [run(): pl.pallas_call(body, out_shape=jax.ShapeDtypeStruct((TOK_SEQ, COLS), BF16...]
    neg x1 -> x0, other arithmetic: 1.73 us -> none  [rope_tables(): -sine]
    unnamed x0 -> x1, local copies, waits for them, and re-layouts: none -> 1.64 us
where the time goes in v3:
time: 130 us
  Pallas kernels  128 us (98%)
  local copies, waits for them, and re-layouts  1.64 us (1%)
    pallas_call x1, Pallas kernels, run(): pl.pallas_call(body, out_shape=jax.ShapeDtypeStruct((COLS, TOK_SEQ), BF16...  128 us

profile of v3, /device:TPU:96, one launch (start us, length us, event | category | flops | bytes accessed | tf_op | source)
XLA Modules:
  0.0 129.5 jit_solution(14197731103853167801)
XLA Ops:
  0.0 127.9 %block.1 = bf16[224,512]{1,0:T(8,128)(2,1)} custom-call(s32[3,256]{1,0:T(4,128)} %bitcast.7, bf16[256,1280]{1,0:T(8,128)(2,1)} %patches_hbm.1, f32[1280]{0:T(1024)} %ln_gain.1, f32[1280]{0:T(1024)} %ln_bias.1, bf16[320,5120]{1,0:T(8,128)(2,1)} %bitcast.4, f32[320]{0:T(512)} %up_bias.1, bf16[320,3584]{1,0:T(8,128)(2,1)} %down_hbm.1, f32[3584]{0:T(1024)} %down_bias.1, ...), custom_call_target="tpu_custom_call" | custom-call | tf_op jit(solution)/shard_map/block/pallas_call | solution.py:648
  127.9 1.6 %copy.18 = bf16[512,224]{0,1:T(8,128)(2,1)} copy(bf16[512,224]{0,1:T(8,128)(2,1)} %bitcast.5) | data formatting | bytes 458752

commit v4 on v3

--- a/solution.py
+++ b/solution.py
@@ -164,6 +164,7 @@
 
 ORDER = (0, -1, 1, 2)
 SIGNS = ((1, 0), (-1, 1))
+DIRECT = ((2, 2), (1, 0), (-1, 1))
 HROW = RB // 2
 QROW = RB // 4
 D = HEAD_DIMENSION
@@ -198,7 +199,7 @@
     table, patches_hbm, ln_gain, ln_bias, up_hbm, up_bias, down_hbm, down_bias, text_hbm, gain, q_weight, q_bias,
     kv_weight, kv_bias, o_hbm, frequency, out,
     up, down, o_rows, o_send, o_cols, outgoing, incoming, tokens, lifted, hidden, pa, pb,
-    a_raw, a_mid, a_out, a_sum, b_raw, b_mid, b_out, b_sum, c_raw, c_mid, c_out, shard,
+    a_raw, a_mid, a_out, a_sum, b_raw, b_mid, b_out, b_sum, c_mid, shard,
     rows_ref, weight, normed, query, kv, heads, best, total, acc, pick_ref, cosine, sine, out_turned, out_sum, patches, text, load_sem, send_sem, recv_sem, seq_send, seq_recv,
 ):
     t, x, y = place()
@@ -457,13 +458,11 @@
         along.send(("o", "r", sg), o_region(-sg, 0, part), o_region(-sg, 0, part), at(sg, 0))
         along.send(("o", "c", -sg), o_region(-sg, 0, None), o_region(-sg, 0, None), at(0, 1))
 
-    def a_next(i, part):
-        rows = (pl.ds(0, HROW), pl.ds(0, QROW), pl.ds(QROW, QROW))[0 if part is None else 1 + part]
-        return a_sum.at[wrap(y + i), rows, :]
-
-    def b_next(i, part):
-        rows = (pl.ds(0, HROW), pl.ds(0, QROW), pl.ds(QROW, QROW))[0 if part is None else 1 + part]
-        return b_sum.at[rows, pl.ds(al(wrap(x + i) * BLK, 128), BLK)]
+    def a_next(i):
+        return a_sum.at[wrap(y + i)]
+
+    def b_next(i):
+        return b_sum.at[:, pl.ds(al(wrap(x + i) * BLK, 128), BLK)]
 
     after = ((0, a_next, to_y), (1, b_next, to_x))
     for side, nxt in zip(sides, after):
@@ -474,15 +473,8 @@
         held = a_sum if n == "a" else b_sum
         held[...] = (piece(0, None)[...].astype(F32) + mid[0].astype(F32) + mid[1].astype(F32)).astype(BF16)
         n, piece, to = nxt
-        for sg, part in SIGNS:
-            link.send((n, "raw2", sg), piece(2, part), c_raw.at[n, part], to(sg))
-        for sg, part in SIGNS:
-            link.send((n, "own2", sg), piece(sg, 1 - part), c_mid.at[n, part, 1 - part], to(sg))
-    for n, piece, to in after:
-        for sg, part in SIGNS:
-            link.arrived((n, "raw2", sg), c_raw.at[n, part], to(-sg))
-            c_out[n, part] = (c_raw[n, part].astype(F32) + piece(sg, part)[...].astype(F32)).astype(BF16)
-            link.send((n, "sum2", sg), c_out.at[n, part], c_mid.at[n, part, part], to(sg))
+        for k, (step_to, slot) in enumerate(DIRECT):
+            link.send((n, "direct", k), piece(step_to), c_mid.at[n, slot], to(step_to))
     row = s * TOK_SEQ + y * RB + lax.broadcasted_iota(jnp.int32, (RB, 1), 0)
     image = jnp.zeros((RB, 1), F32)
     for e in range(N_TP):
@@ -490,11 +482,11 @@
     full_bias = row_of(down_bias)
     shift = image * chosen(x, [full_bias[:, k * BLK : (k + 1) * BLK] for k in range(SIDE)])
     for n, piece, to in after:
-        for sg, part in SIGNS:
-            link.arrived((n, "own2", sg), c_mid.at[n, part, 1 - part], to(-sg))
-            link.arrived((n, "sum2", sg), c_mid.at[n, part, part], to(-sg))
-        held = piece(0, None)[...].astype(F32)
-        held = held + c_mid[n, 0].reshape(HROW, BLK).astype(F32) + c_mid[n, 1].reshape(HROW, BLK).astype(F32)
+        for k, (step_to, slot) in enumerate(DIRECT):
+            link.arrived((n, "direct", k), c_mid.at[n, slot], to(-step_to))
+        held = piece(0)[...].astype(F32)
+        for slot in range(3):
+            held = held + c_mid[n, slot].astype(F32)
         shard[pl.ds(n * HROW, HROW), :] = (held + shift[n * HROW : (n + 1) * HROW]).astype(BF16)
 
     for sg, part in SIGNS:
@@ -630,7 +622,7 @@
     along.drain()
 
 
-LINKS = 3 * AG_SEMS + 30 + 24
+LINKS = 3 * AG_SEMS + 30 + 18
 ALONG = 9 + 28
 
 
@@ -658,7 +650,7 @@
             b16(SIDE, HROW, WIDTH), b16(SIDE, HROW, WIDTH),
             b16(2, 2, HROW, BLK), b16(2, SIDE, HROW, BLK), b16(2, 2, HROW, BLK), b16(SIDE, HROW, BLK),
             b16(2, HROW, WIDTH // 2), b16(2, HROW, WIDTH), b16(2, HROW, WIDTH // 2), b16(HROW, WIDTH),
-            b16(2, 2, QROW, BLK), b16(2, 2, 2, QROW, BLK), b16(2, 2, QROW, BLK), b16(RB, BLK),
+            b16(2, 3, HROW, BLK), b16(RB, BLK),
             b16(TOK_SEQ, WIDTH), b16(WIDTH, 3 * D), b16(RB, WIDTH), b16(TOK_SEQ, D), b16(N_SEQ, TOK_SEQ, 2 * D),
             b16(TOK_SEQ, LOCAL_QUERY_HEAD * D), f32(TOK_SEQ, 1), f32(TOK_SEQ, 1), f32(TOK_SEQ, D),
             b16(TOK_SEQ, ROWS), f32(TOK_SEQ, D), f32(TOK_SEQ, D), b16(COLS, LOCAL_QUERY_HEAD * D), f32(COLS, TOK_SEQ),

time: 130 us -> 129 us (level)
  no operation moved by 1% of the time
where the time goes in v4:
time: 129 us
  Pallas kernels  127 us (98%)
  local copies, waits for them, and re-layouts  1.64 us (1%)
    pallas_call x1, Pallas kernels, run(): pl.pallas_call(body, out_shape=jax.ShapeDtypeStruct((COLS, TOK_SEQ), BF16...  127 us

profile of v4, /device:TPU:96, one launch (start us, length us, event | category | flops | bytes accessed | tf_op | source)
XLA Modules:
  0.0 129.1 jit_solution(13563852514529609419)
XLA Ops:
  0.0 127.5 %block.1 = bf16[224,512]{1,0:T(8,128)(2,1)} custom-call(s32[3,256]{1,0:T(4,128)} %bitcast.7, bf16[256,1280]{1,0:T(8,128)(2,1)} %patches_hbm.1, f32[1280]{0:T(1024)} %ln_gain.1, f32[1280]{0:T(1024)} %ln_bias.1, bf16[320,5120]{1,0:T(8,128)(2,1)} %bitcast.4, f32[320]{0:T(512)} %up_bias.1, bf16[320,3584]{1,0:T(8,128)(2,1)} %down_hbm.1, f32[3584]{0:T(1024)} %down_bias.1, ...), custom_call_target="tpu_custom_call" | custom-call | tf_op jit(solution)/shard_map/block/pallas_call | solution.py:640
  127.5 1.6 %copy.18 = bf16[512,224]{0,1:T(8,128)(2,1)} copy(bf16[512,224]{0,1:T(8,128)(2,1)} %bitcast.5) | data formatting | bytes 458752

commit v5 on v4

--- a/solution.py
+++ b/solution.py
@@ -237,17 +237,19 @@
     lane = lax.broadcasted_iota(jnp.int32, (CAP, 4 * CAP), 1)
     token = 2 * lax.rem(slot, 32) + lax.rem(slot // 32 + my_base, 2)
     source = jnp.where(token < my_length, 4 * token, -8)
-    pl.semaphore_wait(barrier, N_TP + 2)
     for i in (1, 2, 3, 0):
         q = wrap(x + i)
         part = jnp.dot((lane == source + q).astype(BF16), fine, preferred_element_type=F32).astype(BF16)
         for u in range(2):
             for r in range(2):
                 outgoing[4 * q + 2 * u + r] = part[r * 32 : (r + 1) * 32, u * TCOL : (u + 1) * TCOL]
+    pl.semaphore_wait(barrier, N_TP + 2)
+    for i in (1, 2, 3, 0):
         for j in (1, 2, 3, 0):
-            if (i, j) != (0, 0):
-                to = at_xy(x + i, y + j)
-                link.send(("a", i, j), outgoing.at[to], incoming.at[t], to)
+            k = (i + j) % SIDE
+            if (k, j) != (0, 0):
+                to = at_xy(x + k, y + j)
+                link.send(("a", k, j), outgoing.at[to], incoming.at[t], to)
     incoming[t] = outgoing[t]
 
     load_o.wait()

time: 129 us -> 126 us (0.977)
  Pallas kernels: 127 us -> 124 us
    pallas_call x1, Pallas kernels: 127 us -> 124 us  [run(): pl.pallas_call(body, out_shape=jax.ShapeDtypeStruct((COLS, TOK_SEQ), BF16...]
where the time goes in v5:
time: 126 us
  Pallas kernels  124 us (98%)
  local copies, waits for them, and re-layouts  1.64 us (1%)
    pallas_call x1, Pallas kernels, run(): pl.pallas_call(body, out_shape=jax.ShapeDtypeStruct((COLS, TOK_SEQ), BF16...  124 us

profile of v5, /device:TPU:96, one launch (start us, length us, event | category | flops | bytes accessed | tf_op | source)
XLA Modules:
  0.0 125.9 jit_solution(10103225006518081133)
XLA Ops:
  0.0 124.3 %block.1 = bf16[224,512]{1,0:T(8,128)(2,1)} custom-call(s32[3,256]{1,0:T(4,128)} %bitcast.7, bf16[256,1280]{1,0:T(8,128)(2,1)} %patches_hbm.1, f32[1280]{0:T(1024)} %ln_gain.1, f32[1280]{0:T(1024)} %ln_bias.1, bf16[320,5120]{1,0:T(8,128)(2,1)} %bitcast.4, f32[320]{0:T(512)} %up_bias.1, bf16[320,3584]{1,0:T(8,128)(2,1)} %down_hbm.1, f32[3584]{0:T(1024)} %down_bias.1, ...), custom_call_target="tpu_custom_call" | custom-call | tf_op jit(solution)/shard_map/block/pallas_call | solution.py:642
  124.3 1.6 %copy.18 = bf16[512,224]{0,1:T(8,128)(2,1)} copy(bf16[512,224]{0,1:T(8,128)(2,1)} %bitcast.5) | data formatting | bytes 458752
